TPU v7x, 256 devices: a whole 4x4x8 slice. The times are simulated.
256 devices in a mesh: slab: 8 (over z), region: 32 (over x, y, core).
Axes of the slice: x: 4, y: 4, z: 8, core: 2. Of those that a mesh axis runs over, the one named last changes fastest.
Arguments:
- prior_matrix: float32 [256, 524288], P('region', 'slab'), may hold values from -6 to 6
- prior_at_measurements: float32 [256, 16384], P('region', 'slab'), may hold values from -6 to 6
- scaled_residual_vector: float32 [256, 16384], P('region', 'slab'), may hold values from -6 to 6
- lattice_coordinates: float32 [2, 524288], P(None, 'slab'), may hold values from 0 to 2
- measurement_coordinates: float32 [2, 16384], replicated, may hold values from 0 to 2
- neighbour_block_totals: int32 [4096], P('slab'), may hold values from 2 to 16, as said below
- neighbour_block_numbers: int32 [4096, 16], P('slab'), may hold values from 0 to 19, as said below
Outputs:
- analysis: float32 [256, 524288], P('region', 'slab')
Inputs may be any that keep to these rules, and one draw needn't show every extreme that they name: neighbour_block_totals[t] observation tiles are listed for grid tile t; in every slab some grid tile lists 16 and some lists 2. `neighbour_block_numbers`: row t's first neighbour_block_totals[t] entries are distinct, and each names an observation tile s * 16 - 2 + e that exists (from 0 to 16 * 8 - 1), s being t's slab; the remaining entries of the row are 0.
All inputs are finite; a program needn't handle non-finite values.
Results may differ from a plain program's by a relative error of at most 0.0003.
Values sent between devices are 32-bit elements; how exact they have to be, the bound alone decides.
No kernel may reach another device: no remote copies, remote signals or barrier semaphores. Data moves between devices by JAX's collectives and lax.ppermute only.
A program may use at most 64 MiB of HBM per device.

v0:
```python
import functools

import functools

import jax
import jax.numpy as jnp
from jax import lax
from jax.experimental import pallas as pl
from jax.experimental.pallas import tpu as pltpu
from jax.sharding import PartitionSpec as P


BLOCK_NODES = 128
OBS_TILE = 128
OBS_SLAB = 16
EDGE = 2
OBS_EXT = OBS_SLAB + 2 * EDGE
RING = 4
OFFSETS = (0, -1, 1, 2)
DEPTH = 6


def region_shift(block, dx, dy, dc):
    pairs = []
    for source in range(RING * RING * 2):
        x, y, c = source // 8, (source // 2) % 4, source % 2
        pairs.append((source, ((x + dx) % 4) * 8 + ((y + dy) % 4) * 2 + (c ^ dc)))
    return lax.ppermute(block, "region", pairs)


def ring_pieces(block, dx, dy):
    return [
        block,
        region_shift(block, dx, dy, 0),
        region_shift(block, -dx, -dy, 0),
        region_shift(block, 2 * dx, 2 * dy, 0),
    ]


COUNT, ORDER_A, ORDER_B, MINE = 512, 544, 576, 608


def pack_kernel(me, order, totals, listed, tiles, packed, plan):
    def copy(p, carry):
        packed[p] = tiles[order[p]]
        return carry

    lax.fori_loop(0, packed.shape[0], copy, 0, unroll=16)
    region = me[0]
    slots = order.shape[0] // 32

    def tile_plan(slot, count):
        tile = order[region * slots + slot]
        plan[MINE + slot] = tile
        total = totals[tile]

        def group(g, count):
            second = 2 * g + 1
            plan[count] = slot
            plan[128 + count] = listed[2 * g, tile]
            plan[256 + count] = listed[jnp.minimum(second, total - 1), tile]
            plan[384 + count] = jnp.where(second < total, 2, 1)
            return count + 1

        return lax.fori_loop(0, lax.div(total + 1, 2), group, count)

    plan[COUNT] = 0
    count = 0
    for half in range(2):
        count = lax.fori_loop(half * slots // 2, (half + 1) * slots // 2, tile_plan, count)
        odd = count & 1

        @pl.when(odd == 1)
        def _(count=count, half=half):
            plan[count] = (half + 1) * slots // 2 - 1
            plan[128 + count] = plan[128 + count - 1]
            plan[256 + count] = plan[256 + count - 1]
            plan[384 + count] = 0

        count = count + odd
        plan[COUNT + 1 + half] = count

    x, y, c = lax.shift_right_logical(region, 3), lax.shift_right_logical(region, 1) & 3, region & 1
    for b in range(32):
        core = (c + b // 16) & 1
        outer, inner = OFFSETS[(b // 4) % 4], OFFSETS[b % 4]
        plan[ORDER_A + b] = ((x + inner) & 3) * 8 + ((y + outer) & 3) * 2 + core
        plan[ORDER_B + b] = ((x + outer) & 3) * 8 + ((y + inner) & 3) * 2 + core


def taper_of(dx, dy):
    square = jnp.maximum(dx * dx + dy * dy, 1e-30)
    inverse = lax.rsqrt(square)
    z = square * inverse
    near = square * (z * (z * (-0.25 * z + 0.5) + 0.625) - 5.0 / 3.0) + 1.0
    far = (
        z * (z * (z * (z * (z * (1.0 / 12.0) - 0.5) + 0.625) + 5.0 / 3.0) - 5.0)
        + 4.0
        - (2.0 / 3.0) * inverse
    )
    return jnp.where(z <= 1.0, near, jnp.where(z <= 2.0, far, 0.0))


def halves(value):
    high = value.astype(jnp.bfloat16)
    low = (value - high.astype(jnp.float32)).astype(jnp.bfloat16)
    return high, low


def taper_kernel(me, plan, lattice, obs_xy, tapers, place_x, place_y, held, sent):
    count = plan[COUNT + 2]
    depth = held.shape[0]

    def place(q, carry):
        tile = me[1] * OBS_SLAB - EDGE + q
        xy = obs_xy[jnp.minimum(jnp.maximum(tile, 0), obs_xy.shape[0] - 1)]
        place_x[q] = jnp.broadcast_to(xy[0:1], (OBS_TILE, OBS_TILE)).T
        place_y[q] = jnp.broadcast_to(xy[1:2], (OBS_TILE, OBS_TILE)).T
        return carry

    lax.fori_loop(0, OBS_EXT, place, 0)

    def out_copy(i):
        k = lax.rem(i, depth)
        return pltpu.make_async_copy(held.at[k], tapers.at[i], sent.at[k])

    def group(i, carry):
        @pl.when(i >= depth)
        def _():
            out_copy(i - depth).wait()

        slot, q0, q1, keep = plan[i], plan[128 + i], plan[256 + i], plan[384 + i]
        grid_xy = lattice[plan[MINE + slot]]
        grid_x, grid_y = grid_xy[0:1], grid_xy[1:2]
        k = lax.rem(i, depth)
        first = taper_of(grid_x - place_x[q0], grid_y - place_y[q0])
        held[k, :OBS_TILE] = first * jnp.minimum(keep, 1).astype(jnp.float32)
        other = taper_of(grid_x - place_x[q1], grid_y - place_y[q1])
        held[k, OBS_TILE:] = other * jnp.maximum(keep - 1, 0).astype(jnp.float32)
        out_copy(i).start()
        return carry

    lax.fori_loop(0, count, group, 0)

    def drain(i, carry):
        out_copy(i).wait()
        return carry

    lax.fori_loop(jnp.maximum(count - depth, 0), count, drain, 0)


def split_kernel(*refs):
    members = 256
    obs, inn, (obs_out, inn_out) = refs[: 2 * RING], refs[2 * RING : 4 * RING], refs[4 * RING :]

    def rows(pieces, q):
        return jnp.concatenate([p[:, q].reshape(8 * RING, OBS_TILE) for p in pieces], axis=0)

    for q in range(obs[0].shape[1]):
        whole = rows(obs, q)
        anom = (whole - jnp.mean(whole, axis=0, keepdims=True)) * (1.0 / (members - 1.0))
        high, low = halves(anom.T)
        obs_out[q, :OBS_TILE] = high
        obs_out[q, OBS_TILE:] = low
        high, low = halves(rows(inn, q))
        inn_out[q, :members] = high
        inn_out[q, members:] = low


def analysis_kernel(
    half, plan, recv, obs_any, inn_any, tapers, out,
    obs, inn, anom, total, weights, held, arrived, loaded,
):
    members = 256
    slots = recv.shape[1]
    start = plan[COUNT + half]
    count = plan[COUNT + half + 1]
    depth = held.shape[0]

    obs_copy = pltpu.make_async_copy(obs_any, obs, loaded.at[0])
    inn_copy = pltpu.make_async_copy(inn_any, inn, loaded.at[1])
    obs_copy.start()
    inn_copy.start()

    def in_copy(i):
        k = lax.rem(i, depth)
        return pltpu.make_async_copy(tapers.at[i], held.at[k], arrived.at[k])

    def first_copy(i, carry):
        in_copy(i).start()
        return carry

    lax.fori_loop(start, jnp.minimum(count, start + depth - 2), first_copy, 0)

    def prepare_tile(slot, carry):
        rows = jnp.concatenate([recv[plan[ORDER_A + b], slot] for b in range(32)], axis=0)
        high, low = halves(rows - jnp.mean(rows, axis=0, keepdims=True))
        anom[slot, :, :BLOCK_NODES] = high
        anom[slot, :, BLOCK_NODES:] = low
        for b in range(32):
            total[slot, 8 * b : 8 * b + 8] = recv[plan[ORDER_B + b], slot]
        return carry

    lax.fori_loop(0, slots, prepare_tile, 0)
    weights[...] = jnp.zeros_like(weights)
    obs_copy.wait()
    inn_copy.wait()

    def add_group(i, k):
        slot, q0, q1 = plan[i] - half * slots, plan[128 + i], plan[256 + i]
        left = jnp.concatenate([inn[q0], inn[q1]], axis=1)
        both = jnp.dot(left, weights[k], preferred_element_type=jnp.float32)
        total[slot] += (
            both[:members, :BLOCK_NODES] + both[:members, BLOCK_NODES:] + both[members:, :BLOCK_NODES]
        )

    def weigh_group(i):
        slot = plan[i] - half * slots
        left = jnp.concatenate([obs[plan[128 + i]], obs[plan[256 + i]]], axis=0)
        both = jnp.dot(left, anom[slot], preferred_element_type=jnp.float32)
        parts = []
        for j in (0, 2 * OBS_TILE):
            top, low = both[j : j + OBS_TILE], both[j + OBS_TILE : j + 2 * OBS_TILE]
            parts.append(top[:, :BLOCK_NODES] + top[:, BLOCK_NODES:] + low[:, :BLOCK_NODES])
        return halves(held[lax.rem(i, depth)] * jnp.concatenate(parts, axis=0))

    def step(n, carry):
        i = start + 2 * n
        for k in range(2):
            @pl.when(i + k + depth - 2 < count)
            def _(k=k):
                in_copy(i + k + depth - 2).start()

        for k in range(2):
            in_copy(i + k).wait()
        before = jnp.maximum(i - 2, start)
        for k in range(2):
            add_group(before + k, k)
        for k in range(2):
            high, low = weigh_group(i + k)
            weights[k, :, :BLOCK_NODES] = high
            weights[k, :, BLOCK_NODES:] = low
        return carry

    lax.fori_loop(0, lax.div(count - start, 2), step, 0)
    for k in range(2):
        add_group(count - 2 + k, k)

    def put(slot, carry):
        for b in range(32):
            out[plan[ORDER_B + b], slot] = total[slot, 8 * b : 8 * b + 8]
        return carry

    lax.fori_loop(0, slots, put, 0)


def unpack_kernel(order, first, second, out):
    slots = first.shape[1]

    def copy(device, carry):
        for half, received in enumerate((first, second)):
            for j in range(slots):
                out[order[(2 * device + half) * slots + j]] = received[device, j]
        return carry

    lax.fori_loop(0, first.shape[0], copy, 0)


VMEM = pl.BlockSpec(memory_space=pltpu.VMEM)
SMEM = pl.BlockSpec(memory_space=pltpu.SMEM)
ANY = pl.BlockSpec(memory_space=pl.ANY)


def per_device(
    prior_matrix,
    prior_at_measurements,
    scaled_residual_vector,
    lattice_coordinates,
    measurement_coordinates,
    neighbour_block_totals,
    neighbour_block_numbers,
):
    regions = lax.axis_size("region")
    slabs = lax.axis_size("slab")
    region = lax.axis_index("region")
    slab = lax.axis_index("slab")
    tiles = neighbour_block_totals.shape[0]
    slots = tiles // regions

    me = jnp.stack((region, slab))

    both = jnp.stack((prior_at_measurements, scaled_residual_vector))
    margin = EDGE * OBS_TILE
    up = [(i, i + 1) for i in range(slabs - 1)]
    low = lax.ppermute(both[:, :, -margin:], "slab", up)
    high = lax.ppermute(both[:, :, :margin], "slab", [(t, s) for s, t in up])

    index = jnp.arange(tiles, dtype=jnp.int32)
    key = neighbour_block_totals * tiles + (tiles - 1 - index)
    rank = jnp.sum((key[None, :] > key[:, None]).astype(jnp.int32), axis=1)
    row, col = rank // regions, rank % regions
    where_to = jnp.where(row % 2 == 0, col, regions - 1 - col) * slots + row
    order = jnp.sum(jnp.where(where_to[None, :] == index[:, None], index[None, :], 0), axis=1)

    packed, plan = pl.pallas_call(
        pack_kernel,
        out_shape=(
            jax.ShapeDtypeStruct((tiles, 8, BLOCK_NODES), jnp.float32),
            jax.ShapeDtypeStruct((640,), jnp.int32),
        ),
        in_specs=[SMEM, SMEM, SMEM, SMEM, VMEM],
        out_specs=(VMEM, SMEM),
        name="pack",
    )(
        me,
        order,
        neighbour_block_totals,
        neighbour_block_numbers.T,
        prior_matrix.reshape(8, tiles, BLOCK_NODES).transpose(1, 0, 2),
    )
    received = lax.all_to_all(packed, "region", split_axis=0, concat_axis=0, tiled=True)

    wide = jnp.concatenate([low, both, high], axis=2)
    wide = wide.reshape(2, 8, OBS_EXT, OBS_TILE).transpose(0, 2, 1, 3)
    obs = jnp.concatenate(ring_pieces(wide[0], 1, 0), axis=0)
    inn = jnp.concatenate(ring_pieces(wide[1], 0, 1), axis=0)
    obs, inn = ring_pieces(obs, 0, 1), ring_pieces(inn, 1, 0)
    obs_other, inn_other = [region_shift(obs[0], 0, 0, 1)], [region_shift(inn[0], 0, 0, 1)]
    for k in range(1, RING):
        obs_other.append(region_shift(obs[k], 0, 0, 1))
        inn_other.append(region_shift(inn[k], 0, 0, 1))
    gathered = [p.reshape(RING, OBS_EXT, 8, OBS_TILE) for p in obs + obs_other + inn + inn_other]

    tapers = pl.pallas_call(
        taper_kernel,
        out_shape=jax.ShapeDtypeStruct((128, 2 * OBS_TILE, BLOCK_NODES), jnp.float32),
        in_specs=[SMEM, SMEM, VMEM, VMEM],
        out_specs=ANY,
        scratch_shapes=[
            pltpu.VMEM((OBS_EXT, OBS_TILE, BLOCK_NODES), jnp.float32),
            pltpu.VMEM((OBS_EXT, OBS_TILE, BLOCK_NODES), jnp.float32),
            pltpu.VMEM((DEPTH, 2 * OBS_TILE, BLOCK_NODES), jnp.float32),
            pltpu.SemaphoreType.DMA((DEPTH,)),
        ],
        cost_estimate=pl.CostEstimate(flops=10**10, bytes_accessed=8 * 2**20, transcendentals=0),
        name="taper",
    )(
        me,
        plan,
        lattice_coordinates.reshape(2, tiles, BLOCK_NODES).transpose(1, 0, 2),
        measurement_coordinates.reshape(2, -1, OBS_TILE).transpose(1, 0, 2),
    )

    part = OBS_EXT // 4
    obs_split, inn_split = pl.pallas_call(
        split_kernel,
        grid=(4,),
        out_shape=(
            jax.ShapeDtypeStruct((OBS_EXT, 2 * OBS_TILE, 256), jnp.bfloat16),
            jax.ShapeDtypeStruct((OBS_EXT, 512, OBS_TILE), jnp.bfloat16),
        ),
        in_specs=[pl.BlockSpec((RING, part, 8, OBS_TILE), lambda i: (0, i, 0, 0))] * 16,
        out_specs=(
            pl.BlockSpec((part, 2 * OBS_TILE, 256), lambda i: (i, 0, 0)),
            pl.BlockSpec((part, 512, OBS_TILE), lambda i: (i, 0, 0)),
        ),
        cost_estimate=pl.CostEstimate(flops=5 * 10**9, bytes_accessed=10 * 2**20, transcendentals=0),
        name="split",
    )(*gathered)

    some = slots // 2
    returned = []
    for half in range(2):
        analysis = pl.pallas_call(
            functools.partial(analysis_kernel, half),
            grid=(1,),
            out_shape=jax.ShapeDtypeStruct((regions, some, 8, BLOCK_NODES), jnp.float32),
            in_specs=[
                SMEM,
                pl.BlockSpec((regions, some, 8, BLOCK_NODES), lambda i, half=half: (0, half, 0, 0)),
                ANY,
                ANY,
                ANY,
            ],
            out_specs=pl.BlockSpec((regions, some, 8, BLOCK_NODES), lambda i: (0, 0, 0, 0)),
            scratch_shapes=[
                pltpu.VMEM((OBS_EXT, 2 * OBS_TILE, 256), jnp.bfloat16),
                pltpu.VMEM((OBS_EXT, 512, OBS_TILE), jnp.bfloat16),
                pltpu.VMEM((some, 256, 2 * BLOCK_NODES), jnp.bfloat16),
                pltpu.VMEM((some, 256, BLOCK_NODES), jnp.float32),
                pltpu.VMEM((2, 256, 2 * BLOCK_NODES), jnp.bfloat16),
                pltpu.VMEM((DEPTH, 2 * OBS_TILE, BLOCK_NODES), jnp.float32),
                pltpu.SemaphoreType.DMA((DEPTH,)),
                pltpu.SemaphoreType.DMA((2,)),
            ],
            cost_estimate=pl.CostEstimate(flops=10**10, bytes_accessed=8 * 2**20, transcendentals=0),
        )(plan, received.reshape(regions, slots, 8, BLOCK_NODES), obs_split, inn_split, tapers)
        returned.append(lax.all_to_all(analysis, "region", split_axis=0, concat_axis=0, tiled=True))
    out = pl.pallas_call(
        unpack_kernel,
        out_shape=jax.ShapeDtypeStruct((tiles, 8, BLOCK_NODES), jnp.float32),
        in_specs=[SMEM, VMEM, VMEM],
        out_specs=VMEM,
        name="unpack",
    )(order, *returned)
    return out.transpose(1, 0, 2).reshape(8, tiles * BLOCK_NODES)


def solution(mesh):
    in_specs = (
        P("region", "slab"),
        P("region", "slab"),
        P("region", "slab"),
        P(None, "slab"),
        P(),
        P("slab"),
        P("slab", None),
    )

    return jax.shard_map(
        per_device, mesh=mesh, in_specs=in_specs, out_specs=P("region", "slab"), check_vma=False
    )
```

profile of v0, /device:TPU:97, one launch (start us, length us, event | category | flops | bytes accessed | tf_op | source)
XLA Modules:
  0.0 176.1 jit_solution(2767271149134030234)
XLA Ops:
  0.0 0.7 pad_maximum_fusion.3
  0.8 4.7 %collective-permute-start = (f32[2,8,256]{2,1,0:T(8,128)S(1)}, f32[2,8,256]{2,1,0:T(8,128)S(1)}, u32[]{:S(2)}, u32[]{:S(2)}) collective-permute-start(f32[2,8,256]{2,1,0:T(8,128)S(1)} %get-tuple-element.15), channel_id=1, source_target_pairs={{0,32},{32,64},{64,96},{96,128},{128,160},{160,192},{192,224},{1,3... | collective-permute-start | bytes 49160 | tf_op jit(solution)/shard_map/ppermute | solution.py:295
  5.5 1.9 %collective-permute-start.1 = (f32[2,8,256]{2,1,0:T(8,128)S(1)}, f32[2,8,256]{2,1,0:T(8,128)S(1)}, u32[]{:S(2)}, u32[]{:S(2)}) collective-permute-start(f32[2,8,256]{2,1,0:T(8,128)S(1)} %get-tuple-element.16), channel_id=1, source_target_pairs={{32,0},{64,32},{96,64},{128,96},{160,128},{192,160},{224,192},{33,... | collective-permute-start | bytes 49160 | tf_op jit(solution)/shard_map/ppermute | solution.py:296
  7.4 0.7 subtract_add_fusion
  8.1 0.2 convert_reduce_fusion
  8.4 2.8 %collective-permute-done.1 = f32[2,8,256]{2,1,0:T(8,128)S(1)} collective-permute-done((f32[2,8,256]{2,1,0:T(8,128)S(1)}, f32[2,8,256]{2,1,0:T(8,128)S(1)}, u32[]{:S(2)}, u32[]{:S(2)}) %collective-permute-start.1) | collective-permute-done | bytes 16416 | tf_op jit(solution)/shard_map/ppermute | solution.py:296
  11.2 0.9 maximum_bitcast_fusion
  12.1 2.8 %collective-permute-start.4 = (f32[20,8,128]{2,1,0:T(8,128)S(1)}, f32[20,8,128]{2,1,0:T(8,128)S(1)}, u32[]{:S(2)}, u32[]{:S(2)}) collective-permute-start(f32[20,8,128]{2,1,0:T(8,128)S(1)} %get-tuple-element.14), channel_id=1, source_target_pairs={{0,16},{1,17},{2,18},{3,19},{4,20},{5,21},{6,22},{7,23},{8,24},{9,... | collective-permute-start | bytes 245768 | tf_op jit(solution)/shard_map/ppermute | solution.py:28
  14.9 0.9 collective-permute-start.3
  15.8 0.6 collective-permute-start.2
  16.4 0.8 select_reduce_fusion.order
  17.2 2.9 %collective-permute-start.14 = (f32[20,8,128]{2,1,0:T(8,128)S(1)}, f32[20,8,128]{2,1,0:T(8,128)S(1)}, u32[]{:S(2)}, u32[]{:S(2)}) collective-permute-start(f32[20,8,128]{2,1,0:T(8,128)S(1)} %get-tuple-element.13), channel_id=1, source_target_pairs={{0,4},{1,5},{2,6},{3,7},{4,0},{5,1},{6,2},{7,3},{8,12},{9,13},{10,... | collective-permute-start | bytes 245768 | tf_op jit(solution)/shard_map/ppermute | solution.py:28
  20.1 0.0 collective-permute-done.4
  20.1 0.5 collective-permute-done.2
  20.7 3.6 %collective-permute-start.8 = (f32[80,8,128]{2,1,0:T(8,128)S(1)}, f32[80,8,128]{2,1,0:T(8,128)S(1)}, u32[]{:S(2)}, u32[]{:S(2)}) collective-permute-start(f32[80,8,128]{2,1,0:T(8,128)S(1)} %pad_maximum_fusion), channel_id=1, source_target_pairs={{0,1},{1,0},{2,3},{3,2},{4,5},{5,4},{6,7},{7,6},{8,9},{9,8},{10,11... | collective-permute-start | bytes 983048 | tf_op jit(solution)/shard_map/ppermute | solution.py:28
  24.2 2.9 %collective-permute-start.7 = (f32[80,8,128]{2,1,0:T(8,128)S(1)}, f32[80,8,128]{2,1,0:T(8,128)}, u32[]{:S(2)}, u32[]{:S(2)}) collective-permute-start(f32[80,8,128]{2,1,0:T(8,128)S(1)} %pad_maximum_fusion), channel_id=1, source_target_pairs={{0,4},{1,5},{2,6},{3,7},{4,0},{5,1},{6,2},{7,3},{8,12},{9,13},{10,... | collective-permute-start | bytes 983048 | tf_op jit(solution)/shard_map/ppermute | solution.py:28
  27.1 0.8 collective-permute-start.6
  27.9 0.7 collective-permute-start.5
  28.6 0.6 pad_add_fusion.me
  29.2 4.8 %pack.1 = (f32[512,8,128]{2,1,0:T(8,128)}, s32[640]{0:T(1024)}) custom-call(s32[2]{0:T(128)} %pad_add_fusion.me, s32[512]{0:T(512)} %select_reduce_fusion.order, s32[512]{0:T(512)} %totals.1, s32[16,512]{1,0:T(8,128)} %bitcast.51, f32[512,8,128]{2,1,0:T(8,128)} %bitcast.42), custom_call_target="tpu_custom_call" | custom-call | tf_op jit(solution)/shard_map/pack/pallas_call | solution.py:305
  34.0 4.8 %all-to-all-start = ((f32[512,8,128]{2,1,0:T(8,128)}), f32[512,8,128]{2,1,0:T(8,128)S(1)}, u32[]{:S(2)}, u32[]{:S(2)}) async-start(f32[512,8,128]{2,1,0:T(8,128)} %get-tuple-element.10), calls=%async_computation | async-start | bytes 4194304 | tf_op jit(solution)/shard_map/all_to_all | solution.py:321
  38.8 2.6 %collective-permute-start.13 = (f32[20,8,128]{2,1,0:T(8,128)S(1)}, f32[20,8,128]{2,1,0:T(8,128)S(1)}, u32[]{:S(2)}, u32[]{:S(2)}) collective-permute-start(f32[20,8,128]{2,1,0:T(8,128)S(1)} %get-tuple-element.13), channel_id=1, source_target_pairs={{0,6},{1,7},{2,0},{3,1},{4,2},{5,3},{6,4},{7,5},{8,14},{9,15},{10,... | collective-permute-start | bytes 245768 | tf_op jit(solution)/shard_map/ppermute | solution.py:28
  41.4 25.9 %collective-permute-done.13 = f32[20,8,128]{2,1,0:T(8,128)S(1)} collective-permute-done((f32[20,8,128]{2,1,0:T(8,128)S(1)}, f32[20,8,128]{2,1,0:T(8,128)S(1)}, u32[]{:S(2)}, u32[]{:S(2)}) %collective-permute-start.13) | collective-permute-done | bytes 81952 | tf_op jit(solution)/shard_map/ppermute | solution.py:28
  67.3 0.6 collective-permute-start.12
  67.9 3.9 %collective-permute-done.12 = f32[20,8,128]{2,1,0:T(8,128)S(1)} collective-permute-done((f32[20,8,128]{2,1,0:T(8,128)S(1)}, f32[20,8,128]{2,1,0:T(8,128)S(1)}, u32[]{:S(2)}, u32[]{:S(2)}) %collective-permute-start.12) | collective-permute-done | bytes 81952 | tf_op jit(solution)/shard_map/ppermute | solution.py:28
  71.8 2.2 %collective-permute-start.18 = (f32[80,8,128]{2,1,0:T(8,128)S(1)}, f32[80,8,128]{2,1,0:T(8,128)S(1)}, u32[]{:S(2)}, u32[]{:S(2)}) collective-permute-start(f32[80,8,128]{2,1,0:T(8,128)S(1)} %pad_maximum_fusion.1), channel_id=1, source_target_pairs={{0,1},{1,0},{2,3},{3,2},{4,5},{5,4},{6,7},{7,6},{8,9},{9,8},{10,11... | collective-permute-start | bytes 983048 | tf_op jit(solution)/shard_map/ppermute | solution.py:28
  74.0 0.5 collective-permute-start.17
  74.6 1.1 collective-permute-start.16
  75.7 0.3 collective-permute-start.15
  76.1 1.0 collective-permute-start.11
  77.0 0.1 collective-permute-start.10
  77.1 7.7 %collective-permute-done.17 = f32[80,8,128]{2,1,0:T(8,128)} collective-permute-done((f32[80,8,128]{2,1,0:T(8,128)S(1)}, f32[80,8,128]{2,1,0:T(8,128)}, u32[]{:S(2)}, u32[]{:S(2)}) %collective-permute-start.17) | collective-permute-done | bytes 327712 | tf_op jit(solution)/shard_map/ppermute | solution.py:28
  84.8 1.5 collective-permute-start.9
  86.4 3.4 %collective-permute-done.16 = f32[80,8,128]{2,1,0:T(8,128)} collective-permute-done((f32[80,8,128]{2,1,0:T(8,128)S(1)}, f32[80,8,128]{2,1,0:T(8,128)}, u32[]{:S(2)}, u32[]{:S(2)}) %collective-permute-start.16) | collective-permute-done | bytes 327712 | tf_op jit(solution)/shard_map/ppermute | solution.py:28
  89.8 1.0 collective-permute-start.21
  90.7 1.6 collective-permute-done.15
  92.3 0.5 collective-permute-start.20
  92.8 0.1 collective-permute-start.19
  92.9 13.6 %taper.1.tapers = f32[128,256,128]{2,1,0:T(8,128)} custom-call(s32[2]{0:T(128)} %pad_add_fusion.me, s32[640]{0:T(1024)} %get-tuple-element.9.plan, f32[512,2,128]{2,1,0:T(2,128)} %bitcast.52, f32[128,2,128]{2,1,0:T(2,128)} %bitcast.56), custom_call_target="tpu_custom_call" | custom-call | flops 10000000000 | bytes 8388608 | tf_op jit(solution)/shard_map/taper/pallas_call | solution.py:334
  106.6 5.9 %split.1 = (bf16[20,256,256]{2,1,0:T(8,128)(2,1)}, bf16[20,512,128]{2,1,0:T(8,128)(2,1)}) custom-call(f32[4,20,8,128]{3,2,1,0:T(8,128)} %bitcast.45, f32[4,20,8,128]{3,2,1,0:T(8,128)} %bitcast.12.refs_1_, f32[4,20,8,128]{3,2,1,0:T(8,128)} %bitcast.13.refs_2_, f32[4,20,8,128]{3,2,1,0:T(8,128)} %bitcast.14.refs_3_, f32[4,20,8,128]{3,2,1,0:T(8,128)} %bitcast.53, ...), custom_call_target="tpu_custom_call" | custom-call | flops 5000000000 | bytes 10485760 | tf_op jit(solution)/shard_map/split/pallas_call | solution.py:355
  112.5 0.0 copy-start.1
  112.5 1.3 copy-done.1
  113.8 15.5 %shard_map.73 = f32[32,8,8,128]{3,2,1,0:T(8,128)} custom-call(s32[640]{0:T(1024)} %get-tuple-element.9.plan, f32[32,16,8,128]{3,2,1,0:T(8,128)} %bitcast.43, bf16[20,256,256]{2,1,0:T(8,128)(2,1)} %get-tuple-element.11.obs_any, bf16[20,512,128]{2,1,0:T(8,128)(2,1)} %get-tuple-element.12.inn_any, f32[128,256,128]{2,1,0:T(8,128)} %taper.1.tapers), custom_call_target="tpu_custom_call" | custom-call | flops 10000000000 | bytes 8388608 | tf_op jit(solution)/shard_map/pallas_call | solution.py:374
  129.4 4.7 %all-to-all-start.1 = ((f32[32,8,8,128]{3,2,1,0:T(8,128)}), f32[32,8,8,128]{3,2,1,0:T(8,128)S(1)}, u32[]{:S(2)}, u32[]{:S(2)}) async-start(f32[32,8,8,128]{3,2,1,0:T(8,128)} %shard_map.73), calls=%async_computation.1 | async-start | bytes 2097152 | tf_op jit(solution)/shard_map/all_to_all | solution.py:398
  134.1 9.8 %shard_map.74 = f32[32,8,8,128]{3,2,1,0:T(8,128)} custom-call(s32[640]{0:T(1024)} %get-tuple-element.9.plan, f32[32,16,8,128]{3,2,1,0:T(8,128)} %bitcast.44, bf16[20,256,256]{2,1,0:T(8,128)(2,1)} %get-tuple-element.11.obs_any, bf16[20,512,128]{2,1,0:T(8,128)(2,1)} %get-tuple-element.12.inn_any, f32[128,256,128]{2,1,0:T(8,128)} %taper.1.tapers), custom_call_target="tpu_custom_call" | custom-call | flops 10000000000 | bytes 8388608 | tf_op jit(solution)/shard_map/pallas_call | solution.py:374
  143.9 7.2 %all-to-all-done.1.first = f32[32,8,8,128]{3,2,1,0:T(8,128)S(1)} async-done(((f32[32,8,8,128]{3,2,1,0:T(8,128)}), f32[32,8,8,128]{3,2,1,0:T(8,128)S(1)}, u32[]{:S(2)}, u32[]{:S(2)}) %all-to-all-start.1) | async-done | bytes 1048608 | tf_op jit(solution)/shard_map/all_to_all | solution.py:398
  151.1 21.4 %all_to_all.15.second = f32[32,8,8,128]{3,2,1,0:T(8,128)} all-to-all(f32[32,8,8,128]{3,2,1,0:T(8,128)} %shard_map.74), channel_id=1, replica_groups=mesh['slab'=8,'region'=32] {'region'}, dimensions={0} | all-to-all | bytes 2097152 | tf_op jit(solution)/shard_map/all_to_all | solution.py:398
  172.5 3.6 %unpack.1 = f32[512,8,128]{2,1,0:T(8,128)} custom-call(s32[512]{0:T(512)} %select_reduce_fusion.order, f32[32,8,8,128]{3,2,1,0:T(8,128)} %copy-done, f32[32,8,8,128]{3,2,1,0:T(8,128)} %all_to_all.15.second), custom_call_target="tpu_custom_call" | custom-call | tf_op jit(solution)/shard_map/unpack/pallas_call | solution.py:399
  (31 shorter events, 0.1 us)
Async XLA Ops:
  0.8 7.7 %collective-permute-start = (f32[2,8,256]{2,1,0:T(8,128)S(1)}, f32[2,8,256]{2,1,0:T(8,128)S(1)}, u32[]{:S(2)}, u32[]{:S(2)}) collective-permute-start(f32[2,8,256]{2,1,0:T(8,128)S(1)} %get-tuple-element.15), channel_id=1, source_target_pairs={{0,32},{32,64},{64,96},{96,128},{128,160},{160,192},{192,224},{1,3... | collective-permute-start | bytes 49160 | tf_op jit(solution)/shard_map/ppermute | solution.py:295
  5.5 5.7 %collective-permute-start.1 = (f32[2,8,256]{2,1,0:T(8,128)S(1)}, f32[2,8,256]{2,1,0:T(8,128)S(1)}, u32[]{:S(2)}, u32[]{:S(2)}) collective-permute-start(f32[2,8,256]{2,1,0:T(8,128)S(1)} %get-tuple-element.16), channel_id=1, source_target_pairs={{32,0},{64,32},{96,64},{128,96},{160,128},{192,160},{224,192},{33,... | collective-permute-start | bytes 49160 | tf_op jit(solution)/shard_map/ppermute | solution.py:296
  12.1 8.0 %collective-permute-start.4 = (f32[20,8,128]{2,1,0:T(8,128)S(1)}, f32[20,8,128]{2,1,0:T(8,128)S(1)}, u32[]{:S(2)}, u32[]{:S(2)}) collective-permute-start(f32[20,8,128]{2,1,0:T(8,128)S(1)} %get-tuple-element.14), channel_id=1, source_target_pairs={{0,16},{1,17},{2,18},{3,19},{4,20},{5,21},{6,22},{7,23},{8,24},{9,... | collective-permute-start | bytes 245768 | tf_op jit(solution)/shard_map/ppermute | solution.py:28
  14.9 5.2 %collective-permute-start.3 = (f32[20,8,128]{2,1,0:T(8,128)S(1)}, f32[20,8,128]{2,1,0:T(8,128)S(1)}, u32[]{:S(2)}, u32[]{:S(2)}) collective-permute-start(f32[20,8,128]{2,1,0:T(8,128)S(1)} %get-tuple-element.14), channel_id=1, source_target_pairs={{0,24},{1,25},{2,26},{3,27},{4,28},{5,29},{6,30},{7,31},{8,0},{9,1... | collective-permute-start | bytes 245768 | tf_op jit(solution)/shard_map/ppermute | solution.py:28
  15.8 4.8 %collective-permute-start.2 = (f32[20,8,128]{2,1,0:T(8,128)S(1)}, f32[20,8,128]{2,1,0:T(8,128)S(1)}, u32[]{:S(2)}, u32[]{:S(2)}) collective-permute-start(f32[20,8,128]{2,1,0:T(8,128)S(1)} %get-tuple-element.14), channel_id=1, source_target_pairs={{0,8},{1,9},{2,10},{3,11},{4,12},{5,13},{6,14},{7,15},{8,16},{9,17... | collective-permute-start | bytes 245768 | tf_op jit(solution)/shard_map/ppermute | solution.py:28
  17.2 21.6 %collective-permute-start.14 = (f32[20,8,128]{2,1,0:T(8,128)S(1)}, f32[20,8,128]{2,1,0:T(8,128)S(1)}, u32[]{:S(2)}, u32[]{:S(2)}) collective-permute-start(f32[20,8,128]{2,1,0:T(8,128)S(1)} %get-tuple-element.13), channel_id=1, source_target_pairs={{0,4},{1,5},{2,6},{3,7},{4,0},{5,1},{6,2},{7,3},{8,12},{9,13},{10,... | collective-permute-start | bytes 245768 | tf_op jit(solution)/shard_map/ppermute | solution.py:28
  20.6 13.4 %copy-start.2 = (f32[80,8,128]{2,1,0:T(8,128)}, f32[80,8,128]{2,1,0:T(8,128)S(1)}, u32[]{:S(2)}) copy-start(f32[80,8,128]{2,1,0:T(8,128)S(1)} %pad_maximum_fusion) | copy-start | bytes 983044
  20.7 53.4 %collective-permute-start.8 = (f32[80,8,128]{2,1,0:T(8,128)S(1)}, f32[80,8,128]{2,1,0:T(8,128)S(1)}, u32[]{:S(2)}, u32[]{:S(2)}) collective-permute-start(f32[80,8,128]{2,1,0:T(8,128)S(1)} %pad_maximum_fusion), channel_id=1, source_target_pairs={{0,1},{1,0},{2,3},{3,2},{4,5},{5,4},{6,7},{7,6},{8,9},{9,8},{10,11... | collective-permute-start | bytes 983048 | tf_op jit(solution)/shard_map/ppermute | solution.py:28
  24.2 50.3 %collective-permute-start.7 = (f32[80,8,128]{2,1,0:T(8,128)S(1)}, f32[80,8,128]{2,1,0:T(8,128)}, u32[]{:S(2)}, u32[]{:S(2)}) collective-permute-start(f32[80,8,128]{2,1,0:T(8,128)S(1)} %pad_maximum_fusion), channel_id=1, source_target_pairs={{0,4},{1,5},{2,6},{3,7},{4,0},{5,1},{6,2},{7,3},{8,12},{9,13},{10,... | collective-permute-start | bytes 983048 | tf_op jit(solution)/shard_map/ppermute | solution.py:28
  27.1 48.5 %collective-permute-start.6 = (f32[80,8,128]{2,1,0:T(8,128)S(1)}, f32[80,8,128]{2,1,0:T(8,128)}, u32[]{:S(2)}, u32[]{:S(2)}) collective-permute-start(f32[80,8,128]{2,1,0:T(8,128)S(1)} %pad_maximum_fusion), channel_id=1, source_target_pairs={{0,6},{1,7},{2,0},{3,1},{4,2},{5,3},{6,4},{7,5},{8,14},{9,15},{10,... | collective-permute-start | bytes 983048 | tf_op jit(solution)/shard_map/ppermute | solution.py:28
  27.9 48.1 %collective-permute-start.5 = (f32[80,8,128]{2,1,0:T(8,128)S(1)}, f32[80,8,128]{2,1,0:T(8,128)}, u32[]{:S(2)}, u32[]{:S(2)}) collective-permute-start(f32[80,8,128]{2,1,0:T(8,128)S(1)} %pad_maximum_fusion), channel_id=1, source_target_pairs={{0,2},{1,3},{2,4},{3,5},{4,6},{5,7},{6,0},{7,1},{8,10},{9,11},{10,... | collective-permute-start | bytes 983048 | tf_op jit(solution)/shard_map/ppermute | solution.py:28
  34.0 78.5 %all-to-all-start = ((f32[512,8,128]{2,1,0:T(8,128)}), f32[512,8,128]{2,1,0:T(8,128)S(1)}, u32[]{:S(2)}, u32[]{:S(2)}) async-start(f32[512,8,128]{2,1,0:T(8,128)} %get-tuple-element.10), calls=%async_computation | async-start | bytes 4194304 | tf_op jit(solution)/shard_map/all_to_all | solution.py:321
  38.8 28.5 %collective-permute-start.13 = (f32[20,8,128]{2,1,0:T(8,128)S(1)}, f32[20,8,128]{2,1,0:T(8,128)S(1)}, u32[]{:S(2)}, u32[]{:S(2)}) collective-permute-start(f32[20,8,128]{2,1,0:T(8,128)S(1)} %get-tuple-element.13), channel_id=1, source_target_pairs={{0,6},{1,7},{2,0},{3,1},{4,2},{5,3},{6,4},{7,5},{8,14},{9,15},{10,... | collective-permute-start | bytes 245768 | tf_op jit(solution)/shard_map/ppermute | solution.py:28
  67.3 4.5 %collective-permute-start.12 = (f32[20,8,128]{2,1,0:T(8,128)S(1)}, f32[20,8,128]{2,1,0:T(8,128)S(1)}, u32[]{:S(2)}, u32[]{:S(2)}) collective-permute-start(f32[20,8,128]{2,1,0:T(8,128)S(1)} %get-tuple-element.13), channel_id=1, source_target_pairs={{0,2},{1,3},{2,4},{3,5},{4,6},{5,7},{6,0},{7,1},{8,10},{9,11},{10,... | collective-permute-start | bytes 245768 | tf_op jit(solution)/shard_map/ppermute | solution.py:28
  71.8 34.7 %copy-start.3 = (f32[80,8,128]{2,1,0:T(8,128)}, f32[80,8,128]{2,1,0:T(8,128)S(1)}, u32[]{:S(2)}) copy-start(f32[80,8,128]{2,1,0:T(8,128)S(1)} %pad_maximum_fusion.1) | copy-start | bytes 983044
  71.8 5.2 %collective-permute-start.18 = (f32[80,8,128]{2,1,0:T(8,128)S(1)}, f32[80,8,128]{2,1,0:T(8,128)S(1)}, u32[]{:S(2)}, u32[]{:S(2)}) collective-permute-start(f32[80,8,128]{2,1,0:T(8,128)S(1)} %pad_maximum_fusion.1), channel_id=1, source_target_pairs={{0,1},{1,0},{2,3},{3,2},{4,5},{5,4},{6,7},{7,6},{8,9},{9,8},{10,11... | collective-permute-start | bytes 983048 | tf_op jit(solution)/shard_map/ppermute | solution.py:28
  74.0 32.5 %copy-start.4 = (f32[80,8,128]{2,1,0:T(8,128)}, f32[80,8,128]{2,1,0:T(8,128)S(1)}, u32[]{:S(2)}) copy-start(f32[80,8,128]{2,1,0:T(8,128)S(1)} %collective-permute-done.8) | copy-start | bytes 983044
  74.0 10.8 %collective-permute-start.17 = (f32[80,8,128]{2,1,0:T(8,128)S(1)}, f32[80,8,128]{2,1,0:T(8,128)}, u32[]{:S(2)}, u32[]{:S(2)}) collective-permute-start(f32[80,8,128]{2,1,0:T(8,128)S(1)} %pad_maximum_fusion.1), channel_id=1, source_target_pairs={{0,16},{1,17},{2,18},{3,19},{4,20},{5,21},{6,22},{7,23},{8,24},{9,... | collective-permute-start | bytes 983048 | tf_op jit(solution)/shard_map/ppermute | solution.py:28
  74.6 15.2 %collective-permute-start.16 = (f32[80,8,128]{2,1,0:T(8,128)S(1)}, f32[80,8,128]{2,1,0:T(8,128)}, u32[]{:S(2)}, u32[]{:S(2)}) collective-permute-start(f32[80,8,128]{2,1,0:T(8,128)S(1)} %pad_maximum_fusion.1), channel_id=1, source_target_pairs={{0,24},{1,25},{2,26},{3,27},{4,28},{5,29},{6,30},{7,31},{8,0},{9,1... | collective-permute-start | bytes 983048 | tf_op jit(solution)/shard_map/ppermute | solution.py:28
  75.7 16.6 %collective-permute-start.15 = (f32[80,8,128]{2,1,0:T(8,128)S(1)}, f32[80,8,128]{2,1,0:T(8,128)}, u32[]{:S(2)}, u32[]{:S(2)}) collective-permute-start(f32[80,8,128]{2,1,0:T(8,128)S(1)} %pad_maximum_fusion.1), channel_id=1, source_target_pairs={{0,8},{1,9},{2,10},{3,11},{4,12},{5,13},{6,14},{7,15},{8,16},{9,17... | collective-permute-start | bytes 983048 | tf_op jit(solution)/shard_map/ppermute | solution.py:28
  76.1 16.8 %collective-permute-start.11 = (f32[80,8,128]{2,1,0:T(8,128)}, f32[80,8,128]{2,1,0:T(8,128)S(1)}, u32[]{:S(2)}, u32[]{:S(2)}) collective-permute-start(f32[80,8,128]{2,1,0:T(8,128)} %collective-permute-done.7), channel_id=1, source_target_pairs={{0,1},{1,0},{2,3},{3,2},{4,5},{5,4},{6,7},{7,6},{8,9},{9,8},{10,11... | collective-permute-start | bytes 983048 | tf_op jit(solution)/shard_map/ppermute | solution.py:28
  77.0 15.3 %copy-start.5 = (f32[80,8,128]{2,1,0:T(8,128)}, f32[80,8,128]{2,1,0:T(8,128)S(1)}, u32[]{:S(2)}) copy-start(f32[80,8,128]{2,1,0:T(8,128)S(1)} %collective-permute-done.18) | copy-start | bytes 983044
  77.0 29.6 %collective-permute-start.10 = (f32[80,8,128]{2,1,0:T(8,128)}, f32[80,8,128]{2,1,0:T(8,128)}, u32[]{:S(2)}, u32[]{:S(2)}) collective-permute-start(f32[80,8,128]{2,1,0:T(8,128)} %collective-permute-done.6), channel_id=1, source_target_pairs={{0,1},{1,0},{2,3},{3,2},{4,5},{5,4},{6,7},{7,6},{8,9},{9,8},{10,11... | collective-permute-start | bytes 983048 | tf_op jit(solution)/shard_map/ppermute | solution.py:28
  84.8 21.8 %collective-permute-start.9 = (f32[80,8,128]{2,1,0:T(8,128)}, f32[80,8,128]{2,1,0:T(8,128)}, u32[]{:S(2)}, u32[]{:S(2)}) collective-permute-start(f32[80,8,128]{2,1,0:T(8,128)} %collective-permute-done.5), channel_id=1, source_target_pairs={{0,1},{1,0},{2,3},{3,2},{4,5},{5,4},{6,7},{7,6},{8,9},{9,8},{10,11... | collective-permute-start | bytes 983048 | tf_op jit(solution)/shard_map/ppermute | solution.py:28
  89.8 16.8 %collective-permute-start.21 = (f32[80,8,128]{2,1,0:T(8,128)}, f32[80,8,128]{2,1,0:T(8,128)}, u32[]{:S(2)}, u32[]{:S(2)}) collective-permute-start(f32[80,8,128]{2,1,0:T(8,128)} %collective-permute-done.17), channel_id=1, source_target_pairs={{0,1},{1,0},{2,3},{3,2},{4,5},{5,4},{6,7},{7,6},{8,9},{9,8},{10,11... | collective-permute-start | bytes 983048 | tf_op jit(solution)/shard_map/ppermute | solution.py:28
  92.3 14.3 %collective-permute-start.20 = (f32[80,8,128]{2,1,0:T(8,128)}, f32[80,8,128]{2,1,0:T(8,128)}, u32[]{:S(2)}, u32[]{:S(2)}) collective-permute-start(f32[80,8,128]{2,1,0:T(8,128)} %collective-permute-done.16), channel_id=1, source_target_pairs={{0,1},{1,0},{2,3},{3,2},{4,5},{5,4},{6,7},{7,6},{8,9},{9,8},{10,11... | collective-permute-start | bytes 983048 | tf_op jit(solution)/shard_map/ppermute | solution.py:28
  92.8 13.8 %copy-start.6 = (f32[80,8,128]{2,1,0:T(8,128)}, f32[80,8,128]{2,1,0:T(8,128)S(1)}, u32[]{:S(2)}) copy-start(f32[80,8,128]{2,1,0:T(8,128)S(1)} %collective-permute-done.11) | copy-start | bytes 983044
  92.8 13.8 %collective-permute-start.19 = (f32[80,8,128]{2,1,0:T(8,128)}, f32[80,8,128]{2,1,0:T(8,128)}, u32[]{:S(2)}, u32[]{:S(2)}) collective-permute-start(f32[80,8,128]{2,1,0:T(8,128)} %collective-permute-done.15), channel_id=1, source_target_pairs={{0,1},{1,0},{2,3},{3,2},{4,5},{5,4},{6,7},{7,6},{8,9},{9,8},{10,11... | collective-permute-start | bytes 983048 | tf_op jit(solution)/shard_map/ppermute | solution.py:28
  112.5 1.3 copy-start.1
  129.4 21.8 %all-to-all-start.1 = ((f32[32,8,8,128]{3,2,1,0:T(8,128)}), f32[32,8,8,128]{3,2,1,0:T(8,128)S(1)}, u32[]{:S(2)}, u32[]{:S(2)}) async-start(f32[32,8,8,128]{3,2,1,0:T(8,128)} %shard_map.73), calls=%async_computation.1 | async-start | bytes 2097152 | tf_op jit(solution)/shard_map/all_to_all | solution.py:398
  151.1 21.4 %copy-start = (f32[32,8,8,128]{3,2,1,0:T(8,128)}, f32[32,8,8,128]{3,2,1,0:T(8,128)S(1)}, u32[]{:S(2)}) copy-start(f32[32,8,8,128]{3,2,1,0:T(8,128)S(1)} %all-to-all-done.1.first) | copy-start | bytes 3145732
where the time goes:
time: 177 us; the launch traced here: 176 us
  Pallas kernels  53.2 us (30%)
  waiting for transfers between devices  53 us (30%)
  starting transfers between devices  43 us (24%)
  blocking collectives  21.4 us (12%)
  other arithmetic  3.99 us (2%)
    ppermute x20, waiting for transfers between devices, region_shift(): return lax.ppermute(block, 'region', pairs)  43 us
    ppermute x20, starting transfers between devices, region_shift(): return lax.ppermute(block, 'region', pairs)  26.8 us
    pallas_call x2, Pallas kernels, per_device(): pl.pallas_call(functools.partial(analysis_kernel, half), grid=(1,), out_s...  25.3 us
    all_to_all x1, blocking collectives, per_device(): lax.all_to_all(analysis, 'region', split_axis=0, concat_axis=0, tiled=True)  21.4 us
    pallas_call x1, Pallas kernels, per_device(): pl.pallas_call(taper_kernel, out_shape=jax.ShapeDtypeStruct((128, 2 * OBS...  13.6 us
    all_to_all x1, waiting for transfers between devices, per_device(): lax.all_to_all(analysis, 'region', split_axis=0, concat_axis=0, tiled=True)  7.23 us
    pallas_call x1, Pallas kernels, per_device(): pl.pallas_call(split_kernel, grid=(4,), out_shape=(jax.ShapeDtypeStruct((...  5.87 us
    pallas_call x1, Pallas kernels, per_device(): pl.pallas_call(pack_kernel, out_shape=(jax.ShapeDtypeStruct((tiles, 8, BL...  4.8 us
  transfers between devices with their start and end apart: 24, of which 8 were waited for; matrix products, arithmetic and copies ran while one was open for 1% of the time, Pallas kernels for 19%

commit v1 on v0

v1 whole, which is shorter than its diff:
```python
import functools

import jax
import jax.numpy as jnp
from jax import lax
from jax.experimental import pallas as pl
from jax.experimental.pallas import tpu as pltpu
from jax.sharding import PartitionSpec as P


BLOCK_NODES = 128
OBS_TILE = 128
OBS_SLAB = 16
EDGE = 2
OBS_EXT = OBS_SLAB + 2 * EDGE
RING = 4
OFFSETS = (0, -1, 1, 2)
DEPTH = 6


def region_shift(block, dx, dy, dc):
    pairs = []
    for source in range(RING * RING * 2):
        x, y, c = source // 8, (source // 2) % 4, source % 2
        pairs.append((source, ((x + dx) % 4) * 8 + ((y + dy) % 4) * 2 + (c ^ dc)))
    return lax.ppermute(block, "region", pairs)


def ring_pieces(block, dx, dy):
    return [
        block,
        region_shift(block, dx, dy, 0),
        region_shift(block, -dx, -dy, 0),
        region_shift(block, 2 * dx, 2 * dy, 0),
    ]


COUNT, ORDER_A, ORDER_B, MINE = 512, 544, 576, 608


def pack_kernel(me, order, totals, listed, tiles, packed, plan):
    def copy(p, carry):
        packed[p] = tiles[order[p]]
        return carry

    lax.fori_loop(0, packed.shape[0], copy, 0, unroll=16)
    region = me[0]
    slots = order.shape[0] // 32

    def tile_plan(slot, count):
        tile = order[region * slots + slot]
        plan[MINE + slot] = tile
        total = totals[tile]

        def group(g, count):
            second = 2 * g + 1
            plan[count] = slot
            plan[128 + count] = listed[2 * g, tile]
            plan[256 + count] = listed[jnp.minimum(second, total - 1), tile]
            plan[384 + count] = jnp.where(second < total, 2, 1)
            return count + 1

        return lax.fori_loop(0, lax.div(total + 1, 2), group, count)

    count = lax.fori_loop(0, slots, tile_plan, 0)

    @pl.when(count & 1 == 1)
    def _():
        plan[count] = slots - 1
        plan[128 + count] = plan[128 + count - 1]
        plan[256 + count] = plan[256 + count - 1]
        plan[384 + count] = 0

    plan[COUNT] = count + (count & 1)
    x, y, c = lax.shift_right_logical(region, 3), lax.shift_right_logical(region, 1) & 3, region & 1
    for b in range(32):
        core = (c + b // 16) & 1
        outer, inner = OFFSETS[(b // 4) % 4], OFFSETS[b % 4]
        plan[ORDER_A + b] = ((x + inner) & 3) * 8 + ((y + outer) & 3) * 2 + core
        plan[ORDER_B + b] = ((x + outer) & 3) * 8 + ((y + inner) & 3) * 2 + core


def taper_of(dx, dy):
    square = jnp.maximum(dx * dx + dy * dy, 1e-30)
    inverse = lax.rsqrt(square)
    z = square * inverse
    near = square * (z * (z * (-0.25 * z + 0.5) + 0.625) - 5.0 / 3.0) + 1.0
    beyond = jnp.maximum(z - 1.0, 0.0)
    twice = beyond * beyond
    value = near + (twice * twice) * (beyond * ((2.0 / 3.0) * inverse + 1.0 / 3.0))
    return jnp.where(z <= 2.0, value, 0.0)


def halves(value):
    high = value.astype(jnp.bfloat16)
    low = (value - high.astype(jnp.float32)).astype(jnp.bfloat16)
    return high, low


def taper_kernel(half, me, plan, lattice, obs_xy, *refs):
    tapers, place_x, place_y, held, sent = refs[-5:]
    count = plan[COUNT]
    middle = lax.div(count * 2, 3)
    start, stop = ((0, middle), (middle, count))[half]
    depth = held.shape[0]

    def place(q, carry):
        tile = me[1] * OBS_SLAB - EDGE + q
        xy = obs_xy[jnp.minimum(jnp.maximum(tile, 0), obs_xy.shape[0] - 1)]
        place_x[q] = jnp.broadcast_to(xy[0:1], (OBS_TILE, OBS_TILE)).T
        place_y[q] = jnp.broadcast_to(xy[1:2], (OBS_TILE, OBS_TILE)).T
        return carry

    lax.fori_loop(0, OBS_EXT, place, 0)

    def out_copy(i):
        k = lax.rem(i, depth)
        return pltpu.make_async_copy(held.at[k], tapers.at[i], sent.at[k])

    def group(i, carry):
        @pl.when(i >= start + depth)
        def _():
            out_copy(i - depth).wait()

        slot, q0, q1, keep = plan[i], plan[128 + i], plan[256 + i], plan[384 + i]
        grid_xy = lattice[plan[MINE + slot]]
        grid_x, grid_y = grid_xy[0:1], grid_xy[1:2]
        k = lax.rem(i, depth)
        for j, q in enumerate((q0, q1)):
            away = grid_x + jnp.where(keep > j, 0.0, 16.0)
            rows = pl.ds(j * OBS_TILE, OBS_TILE)
            held[k, rows] = taper_of(away - place_x[q], grid_y - place_y[q])
        out_copy(i).start()
        return carry

    lax.fori_loop(start, stop, group, 0)

    def drain(i, carry):
        out_copy(i).wait()
        return carry

    lax.fori_loop(jnp.maximum(stop - depth, start), stop, drain, 0)


def split_kernel(*refs):
    members = 256
    pieces, (obs_out, inn_out, whole, obs, inn, here, gone) = refs[: 4 * RING], refs[4 * RING :]
    loads = []
    for k, piece in enumerate(pieces):
        place = whole.at[k // (2 * RING), k % (2 * RING)]
        loads.append(pltpu.make_async_copy(piece, place, here.at[k]))
    for load in loads:
        load.start()
    for load in loads:
        load.wait()

    def stores(q):
        return (
            pltpu.make_async_copy(obs.at[q], obs_out.at[q], gone.at[0, q]),
            pltpu.make_async_copy(inn.at[q], inn_out.at[q], gone.at[1, q]),
        )

    def tile(q, carry):
        value = whole[0, :, :, q].reshape(members, OBS_TILE)
        anom = (value - jnp.mean(value, axis=0, keepdims=True)) * (1.0 / (members - 1.0))
        high, low = halves(anom.T)
        obs[q, :OBS_TILE] = high
        obs[q, OBS_TILE:] = low
        high, low = halves(whole[1, :, :, q].reshape(members, OBS_TILE))
        inn[q, :members] = high
        inn[q, members:] = low
        for store in stores(q):
            store.start()
        return carry

    lax.fori_loop(0, OBS_EXT, tile, 0)

    def drain(q, carry):
        for store in stores(q):
            store.wait()
        return carry

    lax.fori_loop(0, OBS_EXT, drain, 0)


def analysis_kernel(
    plan, recv_any, obs_any, inn_any, tapers, out,
    recv, obs, inn, anom, total, weights, held, arrived, loaded,
):
    members = 256
    slots = recv.shape[1]
    count = plan[COUNT]
    depth = held.shape[0]

    recv_copy = pltpu.make_async_copy(recv_any, recv, loaded.at[0])
    obs_copy = pltpu.make_async_copy(obs_any, obs, loaded.at[1])
    inn_copy = pltpu.make_async_copy(inn_any, inn, loaded.at[2])
    for copy in (recv_copy, obs_copy, inn_copy):
        copy.start()

    def in_copy(i):
        k = lax.rem(i, depth)
        return pltpu.make_async_copy(tapers.at[i], held.at[k], arrived.at[k])

    def first_copy(i, carry):
        in_copy(i).start()
        return carry

    lax.fori_loop(0, jnp.minimum(count, depth - 2), first_copy, 0)

    def prepare_tile(slot, carry):
        rows = jnp.concatenate([recv[plan[ORDER_A + b], slot] for b in range(32)], axis=0)
        high, low = halves(rows - jnp.mean(rows, axis=0, keepdims=True))
        anom[slot, :, :BLOCK_NODES] = high
        anom[slot, :, BLOCK_NODES:] = low
        for b in range(32):
            total[slot, 8 * b : 8 * b + 8] = recv[plan[ORDER_B + b], slot]
        return carry

    recv_copy.wait()
    lax.fori_loop(0, slots, prepare_tile, 0)
    weights[...] = jnp.zeros_like(weights)
    obs_copy.wait()
    inn_copy.wait()

    def add_group(i, k):
        slot, q0, q1 = plan[i], plan[128 + i], plan[256 + i]
        left = jnp.concatenate([inn[q0], inn[q1]], axis=1)
        both = jnp.dot(left, weights[k], preferred_element_type=jnp.float32)
        total[slot] += (
            both[:members, :BLOCK_NODES] + both[:members, BLOCK_NODES:] + both[members:, :BLOCK_NODES]
        )

    def weigh_group(i):
        slot = plan[i]
        left = jnp.concatenate([obs[plan[128 + i]], obs[plan[256 + i]]], axis=0)
        both = jnp.dot(left, anom[slot], preferred_element_type=jnp.float32)
        parts = []
        for j in (0, 2 * OBS_TILE):
            top, low = both[j : j + OBS_TILE], both[j + OBS_TILE : j + 2 * OBS_TILE]
            parts.append(top[:, :BLOCK_NODES] + top[:, BLOCK_NODES:] + low[:, :BLOCK_NODES])
        return halves(held[lax.rem(i, depth)] * jnp.concatenate(parts, axis=0))

    def step(n, carry):
        i = 2 * n
        for k in range(2):
            @pl.when(i + k + depth - 2 < count)
            def _(k=k):
                in_copy(i + k + depth - 2).start()

        for k in range(2):
            in_copy(i + k).wait()
        before = jnp.maximum(i - 2, 0)
        for k in range(2):
            add_group(before + k, k)
        for k in range(2):
            high, low = weigh_group(i + k)
            weights[k, :, :BLOCK_NODES] = high
            weights[k, :, BLOCK_NODES:] = low
        return carry

    lax.fori_loop(0, lax.div(count, 2), step, 0)
    for k in range(2):
        add_group(count - 2 + k, k)

    def put(slot, carry):
        for b in range(32):
            out[plan[ORDER_B + b], slot] = total[slot, 8 * b : 8 * b + 8]
        return carry

    lax.fori_loop(0, slots, put, 0)


def unpack_kernel(order, received, out):
    def copy(p, carry):
        out[order[p]] = received[p]
        return carry

    lax.fori_loop(0, received.shape[0], copy, 0, unroll=16)


VMEM = pl.BlockSpec(memory_space=pltpu.VMEM)
SMEM = pl.BlockSpec(memory_space=pltpu.SMEM)
ANY = pl.BlockSpec(memory_space=pl.ANY)


def per_device(
    prior_matrix,
    prior_at_measurements,
    scaled_residual_vector,
    lattice_coordinates,
    measurement_coordinates,
    neighbour_block_totals,
    neighbour_block_numbers,
):
    regions = lax.axis_size("region")
    slabs = lax.axis_size("slab")
    region = lax.axis_index("region")
    slab = lax.axis_index("slab")
    tiles = neighbour_block_totals.shape[0]
    slots = tiles // regions

    me = jnp.stack((region, slab))

    both = jnp.stack((prior_at_measurements, scaled_residual_vector))
    margin = EDGE * OBS_TILE
    up = [(i, i + 1) for i in range(slabs - 1)]
    low = lax.ppermute(both[:, :, -margin:], "slab", up)
    high = lax.ppermute(both[:, :, :margin], "slab", [(t, s) for s, t in up])

    index = jnp.arange(tiles, dtype=jnp.int32)
    key = neighbour_block_totals * tiles + (tiles - 1 - index)
    rank = jnp.sum((key[None, :] > key[:, None]).astype(jnp.int32), axis=1)
    row, col = rank // regions, rank % regions
    where_to = jnp.where(row % 2 == 0, col, regions - 1 - col) * slots + (slots - 1 - row)
    order = jnp.sum(jnp.where(where_to[None, :] == index[:, None], index[None, :], 0), axis=1)

    packed, plan = pl.pallas_call(
        pack_kernel,
        out_shape=(
            jax.ShapeDtypeStruct((tiles, 8, BLOCK_NODES), jnp.float32),
            jax.ShapeDtypeStruct((640,), jnp.int32),
        ),
        in_specs=[SMEM, SMEM, SMEM, SMEM, VMEM],
        out_specs=(VMEM, SMEM),
        name="pack",
    )(
        me,
        order,
        neighbour_block_totals,
        neighbour_block_numbers.T,
        prior_matrix.reshape(8, tiles, BLOCK_NODES).transpose(1, 0, 2),
    )
    received = lax.all_to_all(packed, "region", split_axis=0, concat_axis=0, tiled=True)

    wide = jnp.concatenate([low, both, high], axis=2)
    wide = wide.reshape(2, 8, OBS_EXT, OBS_TILE).transpose(0, 2, 1, 3)
    obs = jnp.concatenate(ring_pieces(wide[0], 1, 0), axis=0)
    inn = jnp.concatenate(ring_pieces(wide[1], 0, 1), axis=0)
    obs, inn = ring_pieces(obs, 0, 1), ring_pieces(inn, 1, 0)
    obs_other, inn_other = [region_shift(obs[0], 0, 0, 1)], [region_shift(inn[0], 0, 0, 1)]
    for k in range(1, RING):
        obs_other.append(region_shift(obs[k], 0, 0, 1))
        inn_other.append(region_shift(inn[k], 0, 0, 1))
    gathered = [p.reshape(RING, OBS_EXT, 8, OBS_TILE) for p in obs + obs_other + inn + inn_other]

    tapers = []
    for half in range(2):
        tapers = [
            pl.pallas_call(
                functools.partial(taper_kernel, half),
                out_shape=jax.ShapeDtypeStruct((128, 2 * OBS_TILE, BLOCK_NODES), jnp.float32),
                in_specs=[SMEM, SMEM, VMEM, VMEM] + [ANY] * len(tapers),
                out_specs=ANY,
                scratch_shapes=[
                    pltpu.VMEM((OBS_EXT, OBS_TILE, BLOCK_NODES), jnp.float32),
                    pltpu.VMEM((OBS_EXT, OBS_TILE, BLOCK_NODES), jnp.float32),
                    pltpu.VMEM((DEPTH, 2 * OBS_TILE, BLOCK_NODES), jnp.float32),
                    pltpu.SemaphoreType.DMA((DEPTH,)),
                ],
                input_output_aliases={4: 0} if tapers else {},
                cost_estimate=pl.CostEstimate(
                    flops=5 * 10**9, bytes_accessed=4 * 2**20, transcendentals=0
                ),
            )(
                me,
                plan,
                lattice_coordinates.reshape(2, tiles, BLOCK_NODES).transpose(1, 0, 2),
                measurement_coordinates.reshape(2, -1, OBS_TILE).transpose(1, 0, 2),
                *tapers,
            )
        ]

    obs_split, inn_split = pl.pallas_call(
        split_kernel,
        out_shape=(
            jax.ShapeDtypeStruct((OBS_EXT, 2 * OBS_TILE, 256), jnp.bfloat16),
            jax.ShapeDtypeStruct((OBS_EXT, 512, OBS_TILE), jnp.bfloat16),
        ),
        in_specs=[ANY] * (4 * RING),
        out_specs=(ANY, ANY),
        scratch_shapes=[
            pltpu.VMEM((2, 2 * RING, RING, OBS_EXT, 8, OBS_TILE), jnp.float32),
            pltpu.VMEM((OBS_EXT, 2 * OBS_TILE, 256), jnp.bfloat16),
            pltpu.VMEM((OBS_EXT, 512, OBS_TILE), jnp.bfloat16),
            pltpu.SemaphoreType.DMA((4 * RING,)),
            pltpu.SemaphoreType.DMA((2, OBS_EXT)),
        ],
        cost_estimate=pl.CostEstimate(flops=5 * 10**9, bytes_accessed=10 * 2**20, transcendentals=0),
        name="split",
    )(*gathered)

    analysis = pl.pallas_call(
        analysis_kernel,
        out_shape=jax.ShapeDtypeStruct((regions, slots, 8, BLOCK_NODES), jnp.float32),
        in_specs=[SMEM] + [ANY] * 4,
        out_specs=VMEM,
        scratch_shapes=[
            pltpu.VMEM((regions, slots, 8, BLOCK_NODES), jnp.float32),
            pltpu.VMEM((OBS_EXT, 2 * OBS_TILE, 256), jnp.bfloat16),
            pltpu.VMEM((OBS_EXT, 512, OBS_TILE), jnp.bfloat16),
            pltpu.VMEM((slots, 256, 2 * BLOCK_NODES), jnp.bfloat16),
            pltpu.VMEM((slots, 256, BLOCK_NODES), jnp.float32),
            pltpu.VMEM((2, 256, 2 * BLOCK_NODES), jnp.bfloat16),
            pltpu.VMEM((DEPTH, 2 * OBS_TILE, BLOCK_NODES), jnp.float32),
            pltpu.SemaphoreType.DMA((DEPTH,)),
            pltpu.SemaphoreType.DMA((3,)),
        ],
        cost_estimate=pl.CostEstimate(flops=2 * 10**10, bytes_accessed=16 * 2**20, transcendentals=0),
        name="analysis",
    )(plan, received.reshape(regions, slots, 8, BLOCK_NODES), obs_split, inn_split, tapers[0])
    returned = lax.all_to_all(
        analysis.reshape(tiles, 8, BLOCK_NODES), "region", split_axis=0, concat_axis=0, tiled=True
    )
    out = pl.pallas_call(
        unpack_kernel,
        out_shape=jax.ShapeDtypeStruct((tiles, 8, BLOCK_NODES), jnp.float32),
        in_specs=[SMEM, VMEM],
        out_specs=VMEM,
        name="unpack",
    )(order, returned)
    return out.transpose(1, 0, 2).reshape(8, tiles * BLOCK_NODES)


def solution(mesh):
    in_specs = (
        P("region", "slab"),
        P("region", "slab"),
        P("region", "slab"),
        P(None, "slab"),
        P(),
        P("slab"),
        P("slab", None),
    )

    return jax.shard_map(
        per_device, mesh=mesh, in_specs=in_specs, out_specs=P("region", "slab"), check_vma=False
    )
```

time: 177 us -> 173 us (0.977)
  the two profiles are of different devices: /device:TPU:97 before, /device:TPU:33 now
where the time goes in v1:
time: 173 us; the launch traced here: 170 us
  Pallas kernels  50.8 us (29%)
  waiting for transfers between devices  41.2 us (24%)
  starting transfers between devices  38.8 us (22%)
  blocking collectives  33.6 us (19%)
  other arithmetic  3.08 us (2%)
  local copies, waits for them, and re-layouts  2.37 us (1%)
    ppermute x20, waiting for transfers between devices, region_shift(): return lax.ppermute(block, 'region', pairs)  41.2 us
    all_to_all x1, blocking collectives, per_device(): lax.all_to_all(analysis.reshape(tiles, 8, BLOCK_NODES), 'region', split_a...  33.6 us
    ppermute x20, starting transfers between devices, region_shift(): return lax.ppermute(block, 'region', pairs)  25 us
    pallas_call x1, Pallas kernels, per_device(): pl.pallas_call(analysis_kernel, out_shape=jax.ShapeDtypeStruct((regions,...  20.1 us
    pallas_call x2, Pallas kernels, per_device(): pl.pallas_call(functools.partial(taper_kernel, half), out_shape=jax.Shape...  15.6 us
    all_to_all x1, starting transfers between devices, per_device(): lax.all_to_all(packed, 'region', split_axis=0, concat_axis=0, tiled=True)  8.31 us
    pallas_call x1, Pallas kernels, per_device(): pl.pallas_call(split_kernel, out_shape=(jax.ShapeDtypeStruct((OBS_EXT, 2...  6.63 us
    pallas_call x1, Pallas kernels, per_device(): pl.pallas_call(pack_kernel, out_shape=(jax.ShapeDtypeStruct((tiles, 8, BL...  4.77 us
  transfers between devices with their start and end apart: 23, of which 7 were waited for; matrix products, arithmetic and copies ran while one was open for 1% of the time, Pallas kernels for 16%

profile of v1, /device:TPU:33, one launch (start us, length us, event | category | flops | bytes accessed | tf_op | source)
XLA Modules:
  0.0 170.2 jit_solution(11238738679650915526)
XLA Ops:
  0.0 0.7 pad_maximum_fusion.3
  0.8 3.5 %collective-permute-start = (f32[2,8,256]{2,1,0:T(8,128)S(1)}, f32[2,8,256]{2,1,0:T(8,128)S(1)}, u32[]{:S(2)}, u32[]{:S(2)}) collective-permute-start(f32[2,8,256]{2,1,0:T(8,128)S(1)} %get-tuple-element.15), channel_id=1, source_target_pairs={{0,32},{32,64},{64,96},{96,128},{128,160},{160,192},{192,224},{1,3... | collective-permute-start | bytes 49160 | tf_op jit(solution)/shard_map/ppermute | solution.py:308
  4.3 1.9 %collective-permute-start.1 = (f32[2,8,256]{2,1,0:T(8,128)S(1)}, f32[2,8,256]{2,1,0:T(8,128)S(1)}, u32[]{:S(2)}, u32[]{:S(2)}) collective-permute-start(f32[2,8,256]{2,1,0:T(8,128)S(1)} %get-tuple-element.16), channel_id=1, source_target_pairs={{32,0},{64,32},{96,64},{128,96},{160,128},{192,160},{224,192},{33,... | collective-permute-start | bytes 49160 | tf_op jit(solution)/shard_map/ppermute | solution.py:309
  6.2 0.7 subtract_add_fusion
  6.9 0.2 convert_reduce_fusion
  7.2 0.7 select_reduce_fusion.order
  7.9 0.6 pad_add_fusion.me
  8.5 4.8 %pack.1 = (f32[512,8,128]{2,1,0:T(8,128)}, s32[640]{0:T(1024)}) custom-call(s32[2]{0:T(128)} %pad_add_fusion.me, s32[512]{0:T(512)} %select_reduce_fusion.order, s32[512]{0:T(512)} %totals.1, s32[16,512]{1,0:T(8,128)} %bitcast.56, f32[512,8,128]{2,1,0:T(8,128)} %bitcast.43), custom_call_target="tpu_custom_call" | custom-call | tf_op jit(solution)/shard_map/pack/pallas_call | solution.py:318
  13.3 8.3 %all-to-all-start = ((f32[512,8,128]{2,1,0:T(8,128)}), f32[512,8,128]{2,1,0:T(8,128)S(1)}, u32[]{:S(2)}, u32[]{:S(2)}) async-start(f32[512,8,128]{2,1,0:T(8,128)} %get-tuple-element.10), calls=%async_computation | async-start | bytes 4194304 | tf_op jit(solution)/shard_map/all_to_all | solution.py:334
  21.7 3.0 %collective-permute-start.4 = (f32[20,8,128]{2,1,0:T(8,128)S(1)}, f32[20,8,128]{2,1,0:T(8,128)S(1)}, u32[]{:S(2)}, u32[]{:S(2)}) collective-permute-start(f32[20,8,128]{2,1,0:T(8,128)S(1)} %get-tuple-element.14), channel_id=1, source_target_pairs={{0,16},{1,17},{2,18},{3,19},{4,20},{5,21},{6,22},{7,23},{8,24},{9,... | collective-permute-start | bytes 245768 | tf_op jit(solution)/shard_map/ppermute | solution.py:26
  24.7 0.9 collective-permute-start.3
  25.5 0.6 collective-permute-start.2
  26.1 2.7 %collective-permute-start.14 = (f32[20,8,128]{2,1,0:T(8,128)S(1)}, f32[20,8,128]{2,1,0:T(8,128)S(1)}, u32[]{:S(2)}, u32[]{:S(2)}) collective-permute-start(f32[20,8,128]{2,1,0:T(8,128)S(1)} %get-tuple-element.13), channel_id=1, source_target_pairs={{0,4},{1,5},{2,6},{3,7},{4,0},{5,1},{6,2},{7,3},{8,12},{9,13},{10,... | collective-permute-start | bytes 245768 | tf_op jit(solution)/shard_map/ppermute | solution.py:26
  28.8 20.9 %collective-permute-done.4 = f32[20,8,128]{2,1,0:T(8,128)S(1)} collective-permute-done((f32[20,8,128]{2,1,0:T(8,128)S(1)}, f32[20,8,128]{2,1,0:T(8,128)S(1)}, u32[]{:S(2)}, u32[]{:S(2)}) %collective-permute-start.4) | collective-permute-done | bytes 81952 | tf_op jit(solution)/shard_map/ppermute | solution.py:26
  49.7 0.4 collective-permute-done.3
  50.1 0.9 collective-permute-done.2
  51.0 1.1 collective-permute-start.8
  52.1 2.7 %collective-permute-start.7 = (f32[80,8,128]{2,1,0:T(8,128)S(1)}, f32[80,8,128]{2,1,0:T(8,128)S(1)}, u32[]{:S(2)}, u32[]{:S(2)}) collective-permute-start(f32[80,8,128]{2,1,0:T(8,128)S(1)} %pad_maximum_fusion), channel_id=1, source_target_pairs={{0,4},{1,5},{2,6},{3,7},{4,0},{5,1},{6,2},{7,3},{8,12},{9,13},{10,... | collective-permute-start | bytes 983048 | tf_op jit(solution)/shard_map/ppermute | solution.py:26
  54.8 0.9 collective-permute-start.6
  55.7 0.6 collective-permute-start.5
  56.3 2.1 %collective-permute-start.13 = (f32[20,8,128]{2,1,0:T(8,128)S(1)}, f32[20,8,128]{2,1,0:T(8,128)S(1)}, u32[]{:S(2)}, u32[]{:S(2)}) collective-permute-start(f32[20,8,128]{2,1,0:T(8,128)S(1)} %get-tuple-element.13), channel_id=1, source_target_pairs={{0,6},{1,7},{2,0},{3,1},{4,2},{5,3},{6,4},{7,5},{8,14},{9,15},{10,... | collective-permute-start | bytes 245768 | tf_op jit(solution)/shard_map/ppermute | solution.py:26
  58.3 13.3 %collective-permute-done.13 = f32[20,8,128]{2,1,0:T(8,128)S(1)} collective-permute-done((f32[20,8,128]{2,1,0:T(8,128)S(1)}, f32[20,8,128]{2,1,0:T(8,128)S(1)}, u32[]{:S(2)}, u32[]{:S(2)}) %collective-permute-start.13) | collective-permute-done | bytes 81952 | tf_op jit(solution)/shard_map/ppermute | solution.py:26
  71.6 1.6 collective-permute-start.12
  73.2 3.1 %collective-permute-done.12 = f32[20,8,128]{2,1,0:T(8,128)S(1)} collective-permute-done((f32[20,8,128]{2,1,0:T(8,128)S(1)}, f32[20,8,128]{2,1,0:T(8,128)S(1)}, u32[]{:S(2)}, u32[]{:S(2)}) %collective-permute-start.12) | collective-permute-done | bytes 81952 | tf_op jit(solution)/shard_map/ppermute | solution.py:26
  76.3 2.0 %collective-permute-start.18 = (f32[80,8,128]{2,1,0:T(8,128)S(1)}, f32[80,8,128]{2,1,0:T(8,128)}, u32[]{:S(2)}, u32[]{:S(2)}) collective-permute-start(f32[80,8,128]{2,1,0:T(8,128)S(1)} %pad_maximum_fusion.1), channel_id=1, source_target_pairs={{0,1},{1,0},{2,3},{3,2},{4,5},{5,4},{6,7},{7,6},{8,9},{9,8},{10,11... | collective-permute-start | bytes 983048 | tf_op jit(solution)/shard_map/ppermute | solution.py:26
  78.3 1.7 collective-permute-start.17
  80.0 0.6 collective-permute-start.16
  80.7 0.8 collective-permute-start.15
  81.5 1.0 collective-permute-start.11
  82.6 9.1 %shard_map.73.refs_0_ = f32[128,256,128]{2,1,0:T(8,128)} custom-call(s32[2]{0:T(128)} %pad_add_fusion.me, s32[640]{0:T(1024)} %get-tuple-element.9.plan, f32[512,2,128]{2,1,0:T(2,128)} %bitcast.46, f32[128,2,128]{2,1,0:T(2,128)} %bitcast.54), custom_call_target="tpu_custom_call" | custom-call | flops 5000000000 | bytes 4194304 | tf_op jit(solution)/shard_map/pallas_call | solution.py:350
  91.7 1.0 collective-permute-start.10
  92.7 0.3 collective-permute-start.9
  93.0 1.6 collective-permute-done.16
  94.5 1.0 collective-permute-start.21
  95.5 1.1 collective-permute-done.15
  96.6 0.5 collective-permute-start.20
  97.1 0.0 collective-permute-start.19
  97.1 6.6 %shard_map.74.tapers = f32[128,256,128]{2,1,0:T(8,128)} custom-call(s32[2]{0:T(128)} %pad_add_fusion.me, s32[640]{0:T(1024)} %get-tuple-element.9.plan, f32[512,2,128]{2,1,0:T(2,128)} %bitcast.47, f32[128,2,128]{2,1,0:T(2,128)} %bitcast.55, f32[128,256,128]{2,1,0:T(8,128)} %shard_map.73.refs_0_), custom_call_target="tpu_custom_call", output_to_operand_aliasing={{}: (4, {})} | custom-call | flops 5000000000 | bytes 4194304 | tf_op jit(solution)/shard_map/pallas_call | solution.py:350
  103.8 0.6 copy-done.9
  104.4 0.1 copy-done.10
  104.6 0.2 copy-done.11
  104.7 0.1 copy-done.12
  104.8 6.6 %split.1 = (bf16[20,256,256]{2,1,0:T(8,128)(2,1)}, bf16[20,512,128]{2,1,0:T(8,128)(2,1)}) custom-call(f32[4,20,8,128]{3,2,1,0:T(8,128)} %bitcast.48, f32[4,20,8,128]{3,2,1,0:T(8,128)} %bitcast.60, f32[4,20,8,128]{3,2,1,0:T(8,128)} %bitcast.59, f32[4,20,8,128]{3,2,1,0:T(8,128)} %bitcast.58, f32[4,20,8,128]{3,2,1,0:T(8,128)} %bitcast.57, ...), custom_call_target="tpu_custom_call" | custom-call | flops 5000000000 | bytes 10485760 | tf_op jit(solution)/shard_map/split/pallas_call | solution.py:374
  111.4 0.0 copy-start
  111.5 1.3 copy-done
  112.8 20.1 %analysis.1 = f32[32,16,8,128]{3,2,1,0:T(8,128)} custom-call(s32[640]{0:T(1024)} %get-tuple-element.9.plan, f32[32,16,8,128]{3,2,1,0:T(8,128)} %bitcast.44, bf16[20,256,256]{2,1,0:T(8,128)(2,1)} %get-tuple-element.11.obs_any, bf16[20,512,128]{2,1,0:T(8,128)(2,1)} %get-tuple-element.12.inn_any, f32[128,256,128]{2,1,0:T(8,128)} %shard_map.74.tapers), custom_call_target="tpu_custom_call" | custom-call | flops 20000000000 | bytes 16777216 | tf_op jit(solution)/shard_map/analysis/pallas_call | solution.py:393
  132.9 33.6 %all_to_all.10.received = f32[512,8,128]{2,1,0:T(8,128)} all-to-all(f32[512,8,128]{2,1,0:T(8,128)} %bitcast.45), channel_id=1, replica_groups=mesh['slab'=8,'region'=32] {'region'}, dimensions={0} | all-to-all | bytes 4194304 | tf_op jit(solution)/shard_map/all_to_all | solution.py:412
  166.5 3.6 %unpack.1 = f32[512,8,128]{2,1,0:T(8,128)} custom-call(s32[512]{0:T(512)} %select_reduce_fusion.order, f32[512,8,128]{2,1,0:T(8,128)} %all_to_all.10.received), custom_call_target="tpu_custom_call" | custom-call | tf_op jit(solution)/shard_map/unpack/pallas_call | solution.py:415
  (41 shorter events, 0.2 us)
Async XLA Ops:
  0.8 20.9 %collective-permute-start = (f32[2,8,256]{2,1,0:T(8,128)S(1)}, f32[2,8,256]{2,1,0:T(8,128)S(1)}, u32[]{:S(2)}, u32[]{:S(2)}) collective-permute-start(f32[2,8,256]{2,1,0:T(8,128)S(1)} %get-tuple-element.15), channel_id=1, source_target_pairs={{0,32},{32,64},{64,96},{96,128},{128,160},{160,192},{192,224},{1,3... | collective-permute-start | bytes 49160 | tf_op jit(solution)/shard_map/ppermute | solution.py:308
  4.3 17.3 %collective-permute-start.1 = (f32[2,8,256]{2,1,0:T(8,128)S(1)}, f32[2,8,256]{2,1,0:T(8,128)S(1)}, u32[]{:S(2)}, u32[]{:S(2)}) collective-permute-start(f32[2,8,256]{2,1,0:T(8,128)S(1)} %get-tuple-element.16), channel_id=1, source_target_pairs={{32,0},{64,32},{96,64},{128,96},{160,128},{192,160},{224,192},{33,... | collective-permute-start | bytes 49160 | tf_op jit(solution)/shard_map/ppermute | solution.py:309
  13.3 8.4 %copy-start.3 = (f32[8,2048]{1,0:T(8,128)S(1)}, f32[8,2048]{1,0:T(8,128)}, u32[]{:S(2)}) copy-start(f32[8,2048]{1,0:T(8,128)} %param.9) | copy-start | bytes 196612
  13.3 8.4 %copy-start.4 = (f32[8,2048]{1,0:T(8,128)S(1)}, f32[8,2048]{1,0:T(8,128)}, u32[]{:S(2)}) copy-start(f32[8,2048]{1,0:T(8,128)} %param.8) | copy-start | bytes 196612
  13.3 98.1 %all-to-all-start = ((f32[512,8,128]{2,1,0:T(8,128)}), f32[512,8,128]{2,1,0:T(8,128)S(1)}, u32[]{:S(2)}, u32[]{:S(2)}) async-start(f32[512,8,128]{2,1,0:T(8,128)} %get-tuple-element.10), calls=%async_computation | async-start | bytes 4194304 | tf_op jit(solution)/shard_map/all_to_all | solution.py:334
  21.7 28.0 %collective-permute-start.4 = (f32[20,8,128]{2,1,0:T(8,128)S(1)}, f32[20,8,128]{2,1,0:T(8,128)S(1)}, u32[]{:S(2)}, u32[]{:S(2)}) collective-permute-start(f32[20,8,128]{2,1,0:T(8,128)S(1)} %get-tuple-element.14), channel_id=1, source_target_pairs={{0,16},{1,17},{2,18},{3,19},{4,20},{5,21},{6,22},{7,23},{8,24},{9,... | collective-permute-start | bytes 245768 | tf_op jit(solution)/shard_map/ppermute | solution.py:26
  24.7 25.5 %collective-permute-start.3 = (f32[20,8,128]{2,1,0:T(8,128)S(1)}, f32[20,8,128]{2,1,0:T(8,128)S(1)}, u32[]{:S(2)}, u32[]{:S(2)}) collective-permute-start(f32[20,8,128]{2,1,0:T(8,128)S(1)} %get-tuple-element.14), channel_id=1, source_target_pairs={{0,24},{1,25},{2,26},{3,27},{4,28},{5,29},{6,30},{7,31},{8,0},{9,1... | collective-permute-start | bytes 245768 | tf_op jit(solution)/shard_map/ppermute | solution.py:26
  25.5 25.4 %collective-permute-start.2 = (f32[20,8,128]{2,1,0:T(8,128)S(1)}, f32[20,8,128]{2,1,0:T(8,128)S(1)}, u32[]{:S(2)}, u32[]{:S(2)}) collective-permute-start(f32[20,8,128]{2,1,0:T(8,128)S(1)} %get-tuple-element.14), channel_id=1, source_target_pairs={{0,8},{1,9},{2,10},{3,11},{4,12},{5,13},{6,14},{7,15},{8,16},{9,17... | collective-permute-start | bytes 245768 | tf_op jit(solution)/shard_map/ppermute | solution.py:26
  26.1 30.1 %collective-permute-start.14 = (f32[20,8,128]{2,1,0:T(8,128)S(1)}, f32[20,8,128]{2,1,0:T(8,128)S(1)}, u32[]{:S(2)}, u32[]{:S(2)}) collective-permute-start(f32[20,8,128]{2,1,0:T(8,128)S(1)} %get-tuple-element.13), channel_id=1, source_target_pairs={{0,4},{1,5},{2,6},{3,7},{4,0},{5,1},{6,2},{7,3},{8,12},{9,13},{10,... | collective-permute-start | bytes 245768 | tf_op jit(solution)/shard_map/ppermute | solution.py:26
  51.0 40.6 %copy-start.1 = (f32[80,8,128]{2,1,0:T(8,128)}, f32[80,8,128]{2,1,0:T(8,128)S(1)}, u32[]{:S(2)}) copy-start(f32[80,8,128]{2,1,0:T(8,128)S(1)} %pad_maximum_fusion) | copy-start | bytes 983044
  51.0 27.3 %collective-permute-start.8 = (f32[80,8,128]{2,1,0:T(8,128)S(1)}, f32[80,8,128]{2,1,0:T(8,128)S(1)}, u32[]{:S(2)}, u32[]{:S(2)}) collective-permute-start(f32[80,8,128]{2,1,0:T(8,128)S(1)} %pad_maximum_fusion), channel_id=1, source_target_pairs={{0,1},{1,0},{2,3},{3,2},{4,5},{5,4},{6,7},{7,6},{8,9},{9,8},{10,11... | collective-permute-start | bytes 983048 | tf_op jit(solution)/shard_map/ppermute | solution.py:26
  52.1 28.0 %collective-permute-start.7 = (f32[80,8,128]{2,1,0:T(8,128)S(1)}, f32[80,8,128]{2,1,0:T(8,128)S(1)}, u32[]{:S(2)}, u32[]{:S(2)}) collective-permute-start(f32[80,8,128]{2,1,0:T(8,128)S(1)} %pad_maximum_fusion), channel_id=1, source_target_pairs={{0,4},{1,5},{2,6},{3,7},{4,0},{5,1},{6,2},{7,3},{8,12},{9,13},{10,... | collective-permute-start | bytes 983048 | tf_op jit(solution)/shard_map/ppermute | solution.py:26
  54.8 25.9 %collective-permute-start.6 = (f32[80,8,128]{2,1,0:T(8,128)S(1)}, f32[80,8,128]{2,1,0:T(8,128)S(1)}, u32[]{:S(2)}, u32[]{:S(2)}) collective-permute-start(f32[80,8,128]{2,1,0:T(8,128)S(1)} %pad_maximum_fusion), channel_id=1, source_target_pairs={{0,6},{1,7},{2,0},{3,1},{4,2},{5,3},{6,4},{7,5},{8,14},{9,15},{10,... | collective-permute-start | bytes 983048 | tf_op jit(solution)/shard_map/ppermute | solution.py:26
  55.7 25.8 %collective-permute-start.5 = (f32[80,8,128]{2,1,0:T(8,128)S(1)}, f32[80,8,128]{2,1,0:T(8,128)S(1)}, u32[]{:S(2)}, u32[]{:S(2)}) collective-permute-start(f32[80,8,128]{2,1,0:T(8,128)S(1)} %pad_maximum_fusion), channel_id=1, source_target_pairs={{0,2},{1,3},{2,4},{3,5},{4,6},{5,7},{6,0},{7,1},{8,10},{9,11},{10,... | collective-permute-start | bytes 983048 | tf_op jit(solution)/shard_map/ppermute | solution.py:26
  56.3 15.3 %collective-permute-start.13 = (f32[20,8,128]{2,1,0:T(8,128)S(1)}, f32[20,8,128]{2,1,0:T(8,128)S(1)}, u32[]{:S(2)}, u32[]{:S(2)}) collective-permute-start(f32[20,8,128]{2,1,0:T(8,128)S(1)} %get-tuple-element.13), channel_id=1, source_target_pairs={{0,6},{1,7},{2,0},{3,1},{4,2},{5,3},{6,4},{7,5},{8,14},{9,15},{10,... | collective-permute-start | bytes 245768 | tf_op jit(solution)/shard_map/ppermute | solution.py:26
  71.6 4.7 %collective-permute-start.12 = (f32[20,8,128]{2,1,0:T(8,128)S(1)}, f32[20,8,128]{2,1,0:T(8,128)S(1)}, u32[]{:S(2)}, u32[]{:S(2)}) collective-permute-start(f32[20,8,128]{2,1,0:T(8,128)S(1)} %get-tuple-element.13), channel_id=1, source_target_pairs={{0,2},{1,3},{2,4},{3,5},{4,6},{5,7},{6,0},{7,1},{8,10},{9,11},{10,... | collective-permute-start | bytes 245768 | tf_op jit(solution)/shard_map/ppermute | solution.py:26
  76.3 15.4 %copy-start.2 = (f32[80,8,128]{2,1,0:T(8,128)}, f32[80,8,128]{2,1,0:T(8,128)S(1)}, u32[]{:S(2)}) copy-start(f32[80,8,128]{2,1,0:T(8,128)S(1)} %pad_maximum_fusion.1) | copy-start | bytes 983044
  76.3 15.4 %collective-permute-start.18 = (f32[80,8,128]{2,1,0:T(8,128)S(1)}, f32[80,8,128]{2,1,0:T(8,128)}, u32[]{:S(2)}, u32[]{:S(2)}) collective-permute-start(f32[80,8,128]{2,1,0:T(8,128)S(1)} %pad_maximum_fusion.1), channel_id=1, source_target_pairs={{0,1},{1,0},{2,3},{3,2},{4,5},{5,4},{6,7},{7,6},{8,9},{9,8},{10,11... | collective-permute-start | bytes 983048 | tf_op jit(solution)/shard_map/ppermute | solution.py:26
  78.3 13.3 %copy-start.5 = (f32[80,8,128]{2,1,0:T(8,128)}, f32[80,8,128]{2,1,0:T(8,128)S(1)}, u32[]{:S(2)}) copy-start(f32[80,8,128]{2,1,0:T(8,128)S(1)} %collective-permute-done.8) | copy-start | bytes 983044
  78.3 14.3 %collective-permute-start.17 = (f32[80,8,128]{2,1,0:T(8,128)S(1)}, f32[80,8,128]{2,1,0:T(8,128)}, u32[]{:S(2)}, u32[]{:S(2)}) collective-permute-start(f32[80,8,128]{2,1,0:T(8,128)S(1)} %pad_maximum_fusion.1), channel_id=1, source_target_pairs={{0,16},{1,17},{2,18},{3,19},{4,20},{5,21},{6,22},{7,23},{8,24},{9,... | collective-permute-start | bytes 983048 | tf_op jit(solution)/shard_map/ppermute | solution.py:26
  80.0 11.6 %copy-start.6 = (f32[80,8,128]{2,1,0:T(8,128)}, f32[80,8,128]{2,1,0:T(8,128)S(1)}, u32[]{:S(2)}) copy-start(f32[80,8,128]{2,1,0:T(8,128)S(1)} %collective-permute-done.7) | copy-start | bytes 983044
  80.0 14.5 %collective-permute-start.16 = (f32[80,8,128]{2,1,0:T(8,128)S(1)}, f32[80,8,128]{2,1,0:T(8,128)}, u32[]{:S(2)}, u32[]{:S(2)}) collective-permute-start(f32[80,8,128]{2,1,0:T(8,128)S(1)} %pad_maximum_fusion.1), channel_id=1, source_target_pairs={{0,24},{1,25},{2,26},{3,27},{4,28},{5,29},{6,30},{7,31},{8,0},{9,1... | collective-permute-start | bytes 983048 | tf_op jit(solution)/shard_map/ppermute | solution.py:26
  80.7 0.8 copy-start.7
  80.7 15.9 %collective-permute-start.15 = (f32[80,8,128]{2,1,0:T(8,128)S(1)}, f32[80,8,128]{2,1,0:T(8,128)}, u32[]{:S(2)}, u32[]{:S(2)}) collective-permute-start(f32[80,8,128]{2,1,0:T(8,128)S(1)} %pad_maximum_fusion.1), channel_id=1, source_target_pairs={{0,8},{1,9},{2,10},{3,11},{4,12},{5,13},{6,14},{7,15},{8,16},{9,17... | collective-permute-start | bytes 983048 | tf_op jit(solution)/shard_map/ppermute | solution.py:26
  81.5 1.0 copy-start.8
  81.5 15.6 %collective-permute-start.11 = (f32[80,8,128]{2,1,0:T(8,128)S(1)}, f32[80,8,128]{2,1,0:T(8,128)}, u32[]{:S(2)}, u32[]{:S(2)}) collective-permute-start(f32[80,8,128]{2,1,0:T(8,128)S(1)} %collective-permute-done.7), channel_id=1, source_target_pairs={{0,1},{1,0},{2,3},{3,2},{4,5},{5,4},{6,7},{7,6},{8,9},{9,8},{10,11... | collective-permute-start | bytes 983048 | tf_op jit(solution)/shard_map/ppermute | solution.py:26
  91.7 12.0 %collective-permute-start.10 = (f32[80,8,128]{2,1,0:T(8,128)}, f32[80,8,128]{2,1,0:T(8,128)S(1)}, u32[]{:S(2)}, u32[]{:S(2)}) collective-permute-start(f32[80,8,128]{2,1,0:T(8,128)} %copy-done.7), channel_id=1, source_target_pairs={{0,1},{1,0},{2,3},{3,2},{4,5},{5,4},{6,7},{7,6},{8,9},{9,8},{10,11... | collective-permute-start | bytes 983048 | tf_op jit(solution)/shard_map/ppermute | solution.py:26
  92.7 11.0 %collective-permute-start.9 = (f32[80,8,128]{2,1,0:T(8,128)}, f32[80,8,128]{2,1,0:T(8,128)S(1)}, u32[]{:S(2)}, u32[]{:S(2)}) collective-permute-start(f32[80,8,128]{2,1,0:T(8,128)} %copy-done.8), channel_id=1, source_target_pairs={{0,1},{1,0},{2,3},{3,2},{4,5},{5,4},{6,7},{7,6},{8,9},{9,8},{10,11... | collective-permute-start | bytes 983048 | tf_op jit(solution)/shard_map/ppermute | solution.py:26
  94.5 9.2 %collective-permute-start.21 = (f32[80,8,128]{2,1,0:T(8,128)}, f32[80,8,128]{2,1,0:T(8,128)}, u32[]{:S(2)}, u32[]{:S(2)}) collective-permute-start(f32[80,8,128]{2,1,0:T(8,128)} %collective-permute-done.17), channel_id=1, source_target_pairs={{0,1},{1,0},{2,3},{3,2},{4,5},{5,4},{6,7},{7,6},{8,9},{9,8},{10,11... | collective-permute-start | bytes 983048 | tf_op jit(solution)/shard_map/ppermute | solution.py:26
  96.6 7.1 %collective-permute-start.20 = (f32[80,8,128]{2,1,0:T(8,128)}, f32[80,8,128]{2,1,0:T(8,128)S(1)}, u32[]{:S(2)}, u32[]{:S(2)}) collective-permute-start(f32[80,8,128]{2,1,0:T(8,128)} %collective-permute-done.16), channel_id=1, source_target_pairs={{0,1},{1,0},{2,3},{3,2},{4,5},{5,4},{6,7},{7,6},{8,9},{9,8},{10,11... | collective-permute-start | bytes 983048 | tf_op jit(solution)/shard_map/ppermute | solution.py:26
  97.1 6.7 %collective-permute-start.19 = (f32[80,8,128]{2,1,0:T(8,128)}, f32[80,8,128]{2,1,0:T(8,128)S(1)}, u32[]{:S(2)}, u32[]{:S(2)}) collective-permute-start(f32[80,8,128]{2,1,0:T(8,128)} %collective-permute-done.15), channel_id=1, source_target_pairs={{0,1},{1,0},{2,3},{3,2},{4,5},{5,4},{6,7},{7,6},{8,9},{9,8},{10,11... | collective-permute-start | bytes 983048 | tf_op jit(solution)/shard_map/ppermute | solution.py:26
  103.7 0.7 copy-start.9
  103.7 0.8 copy-start.10
  103.8 1.0 copy-start.11
  103.8 1.0 copy-start.12
  111.4 1.3 copy-start

commit v2 on v1

--- a/solution.py
+++ b/solution.py
@@ -35,7 +35,8 @@
     ]
 
 
-COUNT, ORDER_A, ORDER_B, MINE = 512, 544, 576, 608
+GROUPS = 144
+COUNT, ORDER_A, ORDER_B, MINE = 576, 592, 624, 656
 
 
 def pack_kernel(me, order, totals, listed, tiles, packed, plan):
@@ -51,25 +52,21 @@
         tile = order[region * slots + slot]
         plan[MINE + slot] = tile
         total = totals[tile]
-
-        def group(g, count):
-            second = 2 * g + 1
-            plan[count] = slot
-            plan[128 + count] = listed[2 * g, tile]
-            plan[256 + count] = listed[jnp.minimum(second, total - 1), tile]
-            plan[384 + count] = jnp.where(second < total, 2, 1)
-            return count + 1
-
-        return lax.fori_loop(0, lax.div(total + 1, 2), group, count)
+        for g in range(listed.shape[0] // 2):
+            plan[count + g] = slot
+            plan[GROUPS + count + g] = listed[2 * g, tile]
+            plan[2 * GROUPS + count + g] = listed[2 * g + 1, tile]
+            plan[3 * GROUPS + count + g] = jnp.where(2 * g + 1 < total, 2, 1)
+        return count + lax.div(total + 1, 2)
 
     count = lax.fori_loop(0, slots, tile_plan, 0)
 
     @pl.when(count & 1 == 1)
     def _():
         plan[count] = slots - 1
-        plan[128 + count] = plan[128 + count - 1]
-        plan[256 + count] = plan[256 + count - 1]
-        plan[384 + count] = 0
+        plan[GROUPS + count] = plan[GROUPS + count - 1]
+        plan[2 * GROUPS + count] = plan[2 * GROUPS + count - 1]
+        plan[3 * GROUPS + count] = 0
 
     plan[COUNT] = count + (count & 1)
     x, y, c = lax.shift_right_logical(region, 3), lax.shift_right_logical(region, 1) & 3, region & 1
@@ -122,7 +119,7 @@
         def _():
             out_copy(i - depth).wait()
 
-        slot, q0, q1, keep = plan[i], plan[128 + i], plan[256 + i], plan[384 + i]
+        slot, q0, q1, keep = plan[i], plan[GROUPS + i], plan[2 * GROUPS + i], plan[3 * GROUPS + i]
         grid_xy = lattice[plan[MINE + slot]]
         grid_x, grid_y = grid_xy[0:1], grid_xy[1:2]
         k = lax.rem(i, depth)
@@ -224,7 +221,7 @@
     inn_copy.wait()
 
     def add_group(i, k):
-        slot, q0, q1 = plan[i], plan[128 + i], plan[256 + i]
+        slot, q0, q1 = plan[i], plan[GROUPS + i], plan[2 * GROUPS + i]
         left = jnp.concatenate([inn[q0], inn[q1]], axis=1)
         both = jnp.dot(left, weights[k], preferred_element_type=jnp.float32)
         total[slot] += (
@@ -233,7 +230,7 @@
 
     def weigh_group(i):
         slot = plan[i]
-        left = jnp.concatenate([obs[plan[128 + i]], obs[plan[256 + i]]], axis=0)
+        left = jnp.concatenate([obs[plan[GROUPS + i]], obs[plan[2 * GROUPS + i]]], axis=0)
         both = jnp.dot(left, anom[slot], preferred_element_type=jnp.float32)
         parts = []
         for j in (0, 2 * OBS_TILE):
@@ -319,7 +316,7 @@
         pack_kernel,
         out_shape=(
             jax.ShapeDtypeStruct((tiles, 8, BLOCK_NODES), jnp.float32),
-            jax.ShapeDtypeStruct((640,), jnp.int32),
+            jax.ShapeDtypeStruct((768,), jnp.int32),
         ),
         in_specs=[SMEM, SMEM, SMEM, SMEM, VMEM],
         out_specs=(VMEM, SMEM),

time: 173 us -> 172 us (level)
  no operation moved by 1% of the time
where the time goes in v2:
time: 172 us; the launch traced here: 170 us
  Pallas kernels  50.3 us (29%)
  waiting for transfers between devices  41.2 us (24%)
  starting transfers between devices  38.8 us (23%)
  blocking collectives  33.6 us (20%)
  other arithmetic  3.08 us (2%)
  local copies, waits for them, and re-layouts  2.37 us (1%)
    ppermute x20, waiting for transfers between devices, region_shift(): return lax.ppermute(block, 'region', pairs)  41.2 us
    all_to_all x1, blocking collectives, per_device(): lax.all_to_all(analysis.reshape(tiles, 8, BLOCK_NODES), 'region', split_a...  33.6 us
    ppermute x20, starting transfers between devices, region_shift(): return lax.ppermute(block, 'region', pairs)  25 us
    pallas_call x1, Pallas kernels, per_device(): pl.pallas_call(analysis_kernel, out_shape=jax.ShapeDtypeStruct((regions,...  20.1 us
    pallas_call x2, Pallas kernels, per_device(): pl.pallas_call(functools.partial(taper_kernel, half), out_shape=jax.Shape...  15.6 us
    all_to_all x1, starting transfers between devices, per_device(): lax.all_to_all(packed, 'region', split_axis=0, concat_axis=0, tiled=True)  8.28 us
    pallas_call x1, Pallas kernels, per_device(): pl.pallas_call(split_kernel, out_shape=(jax.ShapeDtypeStruct((OBS_EXT, 2...  6.63 us
    pallas_call x1, Pallas kernels, per_device(): pl.pallas_call(pack_kernel, out_shape=(jax.ShapeDtypeStruct((tiles, 8, BL...  4.29 us
  transfers between devices with their start and end apart: 23, of which 7 were waited for; matrix products, arithmetic and copies ran while one was open for 1% of the time, Pallas kernels for 16%

profile of v2, /device:TPU:33, one launch (start us, length us, event | category | flops | bytes accessed | tf_op | source)
XLA Modules:
  0.0 169.7 jit_solution(17945277193951562895)
XLA Ops:
  0.0 0.7 pad_maximum_fusion.3
  0.8 3.5 %collective-permute-start = (f32[2,8,256]{2,1,0:T(8,128)S(1)}, f32[2,8,256]{2,1,0:T(8,128)S(1)}, u32[]{:S(2)}, u32[]{:S(2)}) collective-permute-start(f32[2,8,256]{2,1,0:T(8,128)S(1)} %get-tuple-element.15), channel_id=1, source_target_pairs={{0,32},{32,64},{64,96},{96,128},{128,160},{160,192},{192,224},{1,3... | collective-permute-start | bytes 49160 | tf_op jit(solution)/shard_map/ppermute | solution.py:305
  4.3 1.9 %collective-permute-start.1 = (f32[2,8,256]{2,1,0:T(8,128)S(1)}, f32[2,8,256]{2,1,0:T(8,128)S(1)}, u32[]{:S(2)}, u32[]{:S(2)}) collective-permute-start(f32[2,8,256]{2,1,0:T(8,128)S(1)} %get-tuple-element.16), channel_id=1, source_target_pairs={{32,0},{64,32},{96,64},{128,96},{160,128},{192,160},{224,192},{33,... | collective-permute-start | bytes 49160 | tf_op jit(solution)/shard_map/ppermute | solution.py:306
  6.2 0.7 subtract_add_fusion
  6.9 0.2 convert_reduce_fusion
  7.2 0.7 select_reduce_fusion.order
  7.9 0.6 pad_add_fusion.me
  8.5 4.3 %pack.1 = (f32[512,8,128]{2,1,0:T(8,128)}, s32[768]{0:T(1024)}) custom-call(s32[2]{0:T(128)} %pad_add_fusion.me, s32[512]{0:T(512)} %select_reduce_fusion.order, s32[512]{0:T(512)} %totals.1, s32[16,512]{1,0:T(8,128)} %bitcast.56, f32[512,8,128]{2,1,0:T(8,128)} %bitcast.43), custom_call_target="tpu_custom_call" | custom-call | tf_op jit(solution)/shard_map/pack/pallas_call | solution.py:315
  12.8 0.0 copy-start.3
  12.8 8.3 %all-to-all-start = ((f32[512,8,128]{2,1,0:T(8,128)}), f32[512,8,128]{2,1,0:T(8,128)S(1)}, u32[]{:S(2)}, u32[]{:S(2)}) async-start(f32[512,8,128]{2,1,0:T(8,128)} %get-tuple-element.10), calls=%async_computation | async-start | bytes 4194304 | tf_op jit(solution)/shard_map/all_to_all | solution.py:331
  21.2 3.0 %collective-permute-start.4 = (f32[20,8,128]{2,1,0:T(8,128)S(1)}, f32[20,8,128]{2,1,0:T(8,128)S(1)}, u32[]{:S(2)}, u32[]{:S(2)}) collective-permute-start(f32[20,8,128]{2,1,0:T(8,128)S(1)} %get-tuple-element.14), channel_id=1, source_target_pairs={{0,16},{1,17},{2,18},{3,19},{4,20},{5,21},{6,22},{7,23},{8,24},{9,... | collective-permute-start | bytes 245768 | tf_op jit(solution)/shard_map/ppermute | solution.py:26
  24.2 0.9 collective-permute-start.3
  25.0 0.6 collective-permute-start.2
  25.6 2.7 %collective-permute-start.14 = (f32[20,8,128]{2,1,0:T(8,128)S(1)}, f32[20,8,128]{2,1,0:T(8,128)S(1)}, u32[]{:S(2)}, u32[]{:S(2)}) collective-permute-start(f32[20,8,128]{2,1,0:T(8,128)S(1)} %get-tuple-element.13), channel_id=1, source_target_pairs={{0,4},{1,5},{2,6},{3,7},{4,0},{5,1},{6,2},{7,3},{8,12},{9,13},{10,... | collective-permute-start | bytes 245768 | tf_op jit(solution)/shard_map/ppermute | solution.py:26
  28.3 20.9 %collective-permute-done.4 = f32[20,8,128]{2,1,0:T(8,128)S(1)} collective-permute-done((f32[20,8,128]{2,1,0:T(8,128)S(1)}, f32[20,8,128]{2,1,0:T(8,128)S(1)}, u32[]{:S(2)}, u32[]{:S(2)}) %collective-permute-start.4) | collective-permute-done | bytes 81952 | tf_op jit(solution)/shard_map/ppermute | solution.py:26
  49.2 0.4 collective-permute-done.3
  49.6 0.9 collective-permute-done.2
  50.5 1.1 collective-permute-start.8
  51.6 2.7 %collective-permute-start.7 = (f32[80,8,128]{2,1,0:T(8,128)S(1)}, f32[80,8,128]{2,1,0:T(8,128)S(1)}, u32[]{:S(2)}, u32[]{:S(2)}) collective-permute-start(f32[80,8,128]{2,1,0:T(8,128)S(1)} %pad_maximum_fusion), channel_id=1, source_target_pairs={{0,4},{1,5},{2,6},{3,7},{4,0},{5,1},{6,2},{7,3},{8,12},{9,13},{10,... | collective-permute-start | bytes 983048 | tf_op jit(solution)/shard_map/ppermute | solution.py:26
  54.3 0.9 collective-permute-start.6
  55.2 0.6 collective-permute-start.5
  55.8 2.1 %collective-permute-start.13 = (f32[20,8,128]{2,1,0:T(8,128)S(1)}, f32[20,8,128]{2,1,0:T(8,128)S(1)}, u32[]{:S(2)}, u32[]{:S(2)}) collective-permute-start(f32[20,8,128]{2,1,0:T(8,128)S(1)} %get-tuple-element.13), channel_id=1, source_target_pairs={{0,6},{1,7},{2,0},{3,1},{4,2},{5,3},{6,4},{7,5},{8,14},{9,15},{10,... | collective-permute-start | bytes 245768 | tf_op jit(solution)/shard_map/ppermute | solution.py:26
  57.8 13.3 %collective-permute-done.13 = f32[20,8,128]{2,1,0:T(8,128)S(1)} collective-permute-done((f32[20,8,128]{2,1,0:T(8,128)S(1)}, f32[20,8,128]{2,1,0:T(8,128)S(1)}, u32[]{:S(2)}, u32[]{:S(2)}) %collective-permute-start.13) | collective-permute-done | bytes 81952 | tf_op jit(solution)/shard_map/ppermute | solution.py:26
  71.1 1.6 collective-permute-start.12
  72.7 3.1 %collective-permute-done.12 = f32[20,8,128]{2,1,0:T(8,128)S(1)} collective-permute-done((f32[20,8,128]{2,1,0:T(8,128)S(1)}, f32[20,8,128]{2,1,0:T(8,128)S(1)}, u32[]{:S(2)}, u32[]{:S(2)}) %collective-permute-start.12) | collective-permute-done | bytes 81952 | tf_op jit(solution)/shard_map/ppermute | solution.py:26
  75.8 2.0 %collective-permute-start.18 = (f32[80,8,128]{2,1,0:T(8,128)S(1)}, f32[80,8,128]{2,1,0:T(8,128)}, u32[]{:S(2)}, u32[]{:S(2)}) collective-permute-start(f32[80,8,128]{2,1,0:T(8,128)S(1)} %pad_maximum_fusion.1), channel_id=1, source_target_pairs={{0,1},{1,0},{2,3},{3,2},{4,5},{5,4},{6,7},{7,6},{8,9},{9,8},{10,11... | collective-permute-start | bytes 983048 | tf_op jit(solution)/shard_map/ppermute | solution.py:26
  77.8 1.7 collective-permute-start.17
  79.5 0.6 collective-permute-start.16
  80.2 0.8 collective-permute-start.15
  81.0 1.0 collective-permute-start.11
  82.1 9.1 %shard_map.73.refs_0_ = f32[128,256,128]{2,1,0:T(8,128)} custom-call(s32[2]{0:T(128)} %pad_add_fusion.me, s32[768]{0:T(1024)} %get-tuple-element.9.plan, f32[512,2,128]{2,1,0:T(2,128)} %bitcast.46, f32[128,2,128]{2,1,0:T(2,128)} %bitcast.54), custom_call_target="tpu_custom_call" | custom-call | flops 5000000000 | bytes 4194304 | tf_op jit(solution)/shard_map/pallas_call | solution.py:347
  91.2 1.0 collective-permute-start.10
  92.2 0.3 collective-permute-start.9
  92.5 1.6 collective-permute-done.16
  94.0 1.0 collective-permute-start.21
  95.0 1.1 collective-permute-done.15
  96.1 0.5 collective-permute-start.20
  96.6 0.0 collective-permute-start.19
  96.6 6.6 %shard_map.74.tapers = f32[128,256,128]{2,1,0:T(8,128)} custom-call(s32[2]{0:T(128)} %pad_add_fusion.me, s32[768]{0:T(1024)} %get-tuple-element.9.plan, f32[512,2,128]{2,1,0:T(2,128)} %bitcast.47, f32[128,2,128]{2,1,0:T(2,128)} %bitcast.55, f32[128,256,128]{2,1,0:T(8,128)} %shard_map.73.refs_0_), custom_call_target="tpu_custom_call", output_to_operand_aliasing={{}: (4, {})} | custom-call | flops 5000000000 | bytes 4194304 | tf_op jit(solution)/shard_map/pallas_call | solution.py:347
  103.3 0.6 copy-done.9
  103.9 0.1 copy-done.10
  104.1 0.2 copy-done.11
  104.2 0.1 copy-done.12
  104.3 6.6 %split.1 = (bf16[20,256,256]{2,1,0:T(8,128)(2,1)}, bf16[20,512,128]{2,1,0:T(8,128)(2,1)}) custom-call(f32[4,20,8,128]{3,2,1,0:T(8,128)} %bitcast.48, f32[4,20,8,128]{3,2,1,0:T(8,128)} %bitcast.60, f32[4,20,8,128]{3,2,1,0:T(8,128)} %bitcast.59, f32[4,20,8,128]{3,2,1,0:T(8,128)} %bitcast.58, f32[4,20,8,128]{3,2,1,0:T(8,128)} %bitcast.57, ...), custom_call_target="tpu_custom_call" | custom-call | flops 5000000000 | bytes 10485760 | tf_op jit(solution)/shard_map/split/pallas_call | solution.py:371
  111.0 1.3 copy-done
  112.3 20.1 %analysis.1 = f32[32,16,8,128]{3,2,1,0:T(8,128)} custom-call(s32[768]{0:T(1024)} %get-tuple-element.9.plan, f32[32,16,8,128]{3,2,1,0:T(8,128)} %bitcast.44, bf16[20,256,256]{2,1,0:T(8,128)(2,1)} %get-tuple-element.11.obs_any, bf16[20,512,128]{2,1,0:T(8,128)(2,1)} %get-tuple-element.12.inn_any, f32[128,256,128]{2,1,0:T(8,128)} %shard_map.74.tapers), custom_call_target="tpu_custom_call" | custom-call | flops 20000000000 | bytes 16777216 | tf_op jit(solution)/shard_map/analysis/pallas_call | solution.py:390
  132.4 33.6 %all_to_all.10.received = f32[512,8,128]{2,1,0:T(8,128)} all-to-all(f32[512,8,128]{2,1,0:T(8,128)} %bitcast.45), channel_id=1, replica_groups=mesh['slab'=8,'region'=32] {'region'}, dimensions={0} | all-to-all | bytes 4194304 | tf_op jit(solution)/shard_map/all_to_all | solution.py:409
  166.1 3.6 %unpack.1 = f32[512,8,128]{2,1,0:T(8,128)} custom-call(s32[512]{0:T(512)} %select_reduce_fusion.order, f32[512,8,128]{2,1,0:T(8,128)} %all_to_all.10.received), custom_call_target="tpu_custom_call" | custom-call | tf_op jit(solution)/shard_map/unpack/pallas_call | solution.py:412
  (41 shorter events, 0.2 us)
Async XLA Ops:
  0.8 20.4 %collective-permute-start = (f32[2,8,256]{2,1,0:T(8,128)S(1)}, f32[2,8,256]{2,1,0:T(8,128)S(1)}, u32[]{:S(2)}, u32[]{:S(2)}) collective-permute-start(f32[2,8,256]{2,1,0:T(8,128)S(1)} %get-tuple-element.15), channel_id=1, source_target_pairs={{0,32},{32,64},{64,96},{96,128},{128,160},{160,192},{192,224},{1,3... | collective-permute-start | bytes 49160 | tf_op jit(solution)/shard_map/ppermute | solution.py:305
  4.3 16.8 %collective-permute-start.1 = (f32[2,8,256]{2,1,0:T(8,128)S(1)}, f32[2,8,256]{2,1,0:T(8,128)S(1)}, u32[]{:S(2)}, u32[]{:S(2)}) collective-permute-start(f32[2,8,256]{2,1,0:T(8,128)S(1)} %get-tuple-element.16), channel_id=1, source_target_pairs={{32,0},{64,32},{96,64},{128,96},{160,128},{192,160},{224,192},{33,... | collective-permute-start | bytes 49160 | tf_op jit(solution)/shard_map/ppermute | solution.py:306
  12.8 8.3 %copy-start.3 = (f32[8,2048]{1,0:T(8,128)S(1)}, f32[8,2048]{1,0:T(8,128)}, u32[]{:S(2)}) copy-start(f32[8,2048]{1,0:T(8,128)} %param.9) | copy-start | bytes 196612
  12.8 8.3 %copy-start.4 = (f32[8,2048]{1,0:T(8,128)S(1)}, f32[8,2048]{1,0:T(8,128)}, u32[]{:S(2)}) copy-start(f32[8,2048]{1,0:T(8,128)} %param.8) | copy-start | bytes 196612
  12.8 98.1 %all-to-all-start = ((f32[512,8,128]{2,1,0:T(8,128)}), f32[512,8,128]{2,1,0:T(8,128)S(1)}, u32[]{:S(2)}, u32[]{:S(2)}) async-start(f32[512,8,128]{2,1,0:T(8,128)} %get-tuple-element.10), calls=%async_computation | async-start | bytes 4194304 | tf_op jit(solution)/shard_map/all_to_all | solution.py:331
  21.2 28.0 %collective-permute-start.4 = (f32[20,8,128]{2,1,0:T(8,128)S(1)}, f32[20,8,128]{2,1,0:T(8,128)S(1)}, u32[]{:S(2)}, u32[]{:S(2)}) collective-permute-start(f32[20,8,128]{2,1,0:T(8,128)S(1)} %get-tuple-element.14), channel_id=1, source_target_pairs={{0,16},{1,17},{2,18},{3,19},{4,20},{5,21},{6,22},{7,23},{8,24},{9,... | collective-permute-start | bytes 245768 | tf_op jit(solution)/shard_map/ppermute | solution.py:26
  24.2 25.5 %collective-permute-start.3 = (f32[20,8,128]{2,1,0:T(8,128)S(1)}, f32[20,8,128]{2,1,0:T(8,128)S(1)}, u32[]{:S(2)}, u32[]{:S(2)}) collective-permute-start(f32[20,8,128]{2,1,0:T(8,128)S(1)} %get-tuple-element.14), channel_id=1, source_target_pairs={{0,24},{1,25},{2,26},{3,27},{4,28},{5,29},{6,30},{7,31},{8,0},{9,1... | collective-permute-start | bytes 245768 | tf_op jit(solution)/shard_map/ppermute | solution.py:26
  25.0 25.4 %collective-permute-start.2 = (f32[20,8,128]{2,1,0:T(8,128)S(1)}, f32[20,8,128]{2,1,0:T(8,128)S(1)}, u32[]{:S(2)}, u32[]{:S(2)}) collective-permute-start(f32[20,8,128]{2,1,0:T(8,128)S(1)} %get-tuple-element.14), channel_id=1, source_target_pairs={{0,8},{1,9},{2,10},{3,11},{4,12},{5,13},{6,14},{7,15},{8,16},{9,17... | collective-permute-start | bytes 245768 | tf_op jit(solution)/shard_map/ppermute | solution.py:26
  25.6 30.1 %collective-permute-start.14 = (f32[20,8,128]{2,1,0:T(8,128)S(1)}, f32[20,8,128]{2,1,0:T(8,128)S(1)}, u32[]{:S(2)}, u32[]{:S(2)}) collective-permute-start(f32[20,8,128]{2,1,0:T(8,128)S(1)} %get-tuple-element.13), channel_id=1, source_target_pairs={{0,4},{1,5},{2,6},{3,7},{4,0},{5,1},{6,2},{7,3},{8,12},{9,13},{10,... | collective-permute-start | bytes 245768 | tf_op jit(solution)/shard_map/ppermute | solution.py:26
  50.5 40.6 %copy-start.1 = (f32[80,8,128]{2,1,0:T(8,128)}, f32[80,8,128]{2,1,0:T(8,128)S(1)}, u32[]{:S(2)}) copy-start(f32[80,8,128]{2,1,0:T(8,128)S(1)} %pad_maximum_fusion) | copy-start | bytes 983044
  50.5 27.3 %collective-permute-start.8 = (f32[80,8,128]{2,1,0:T(8,128)S(1)}, f32[80,8,128]{2,1,0:T(8,128)S(1)}, u32[]{:S(2)}, u32[]{:S(2)}) collective-permute-start(f32[80,8,128]{2,1,0:T(8,128)S(1)} %pad_maximum_fusion), channel_id=1, source_target_pairs={{0,1},{1,0},{2,3},{3,2},{4,5},{5,4},{6,7},{7,6},{8,9},{9,8},{10,11... | collective-permute-start | bytes 983048 | tf_op jit(solution)/shard_map/ppermute | solution.py:26
  51.6 28.0 %collective-permute-start.7 = (f32[80,8,128]{2,1,0:T(8,128)S(1)}, f32[80,8,128]{2,1,0:T(8,128)S(1)}, u32[]{:S(2)}, u32[]{:S(2)}) collective-permute-start(f32[80,8,128]{2,1,0:T(8,128)S(1)} %pad_maximum_fusion), channel_id=1, source_target_pairs={{0,4},{1,5},{2,6},{3,7},{4,0},{5,1},{6,2},{7,3},{8,12},{9,13},{10,... | collective-permute-start | bytes 983048 | tf_op jit(solution)/shard_map/ppermute | solution.py:26
  54.3 25.9 %collective-permute-start.6 = (f32[80,8,128]{2,1,0:T(8,128)S(1)}, f32[80,8,128]{2,1,0:T(8,128)S(1)}, u32[]{:S(2)}, u32[]{:S(2)}) collective-permute-start(f32[80,8,128]{2,1,0:T(8,128)S(1)} %pad_maximum_fusion), channel_id=1, source_target_pairs={{0,6},{1,7},{2,0},{3,1},{4,2},{5,3},{6,4},{7,5},{8,14},{9,15},{10,... | collective-permute-start | bytes 983048 | tf_op jit(solution)/shard_map/ppermute | solution.py:26
  55.2 25.8 %collective-permute-start.5 = (f32[80,8,128]{2,1,0:T(8,128)S(1)}, f32[80,8,128]{2,1,0:T(8,128)S(1)}, u32[]{:S(2)}, u32[]{:S(2)}) collective-permute-start(f32[80,8,128]{2,1,0:T(8,128)S(1)} %pad_maximum_fusion), channel_id=1, source_target_pairs={{0,2},{1,3},{2,4},{3,5},{4,6},{5,7},{6,0},{7,1},{8,10},{9,11},{10,... | collective-permute-start | bytes 983048 | tf_op jit(solution)/shard_map/ppermute | solution.py:26
  55.8 15.3 %collective-permute-start.13 = (f32[20,8,128]{2,1,0:T(8,128)S(1)}, f32[20,8,128]{2,1,0:T(8,128)S(1)}, u32[]{:S(2)}, u32[]{:S(2)}) collective-permute-start(f32[20,8,128]{2,1,0:T(8,128)S(1)} %get-tuple-element.13), channel_id=1, source_target_pairs={{0,6},{1,7},{2,0},{3,1},{4,2},{5,3},{6,4},{7,5},{8,14},{9,15},{10,... | collective-permute-start | bytes 245768 | tf_op jit(solution)/shard_map/ppermute | solution.py:26
  71.1 4.7 %collective-permute-start.12 = (f32[20,8,128]{2,1,0:T(8,128)S(1)}, f32[20,8,128]{2,1,0:T(8,128)S(1)}, u32[]{:S(2)}, u32[]{:S(2)}) collective-permute-start(f32[20,8,128]{2,1,0:T(8,128)S(1)} %get-tuple-element.13), channel_id=1, source_target_pairs={{0,2},{1,3},{2,4},{3,5},{4,6},{5,7},{6,0},{7,1},{8,10},{9,11},{10,... | collective-permute-start | bytes 245768 | tf_op jit(solution)/shard_map/ppermute | solution.py:26
  75.8 15.4 %copy-start.2 = (f32[80,8,128]{2,1,0:T(8,128)}, f32[80,8,128]{2,1,0:T(8,128)S(1)}, u32[]{:S(2)}) copy-start(f32[80,8,128]{2,1,0:T(8,128)S(1)} %pad_maximum_fusion.1) | copy-start | bytes 983044
  75.8 15.4 %collective-permute-start.18 = (f32[80,8,128]{2,1,0:T(8,128)S(1)}, f32[80,8,128]{2,1,0:T(8,128)}, u32[]{:S(2)}, u32[]{:S(2)}) collective-permute-start(f32[80,8,128]{2,1,0:T(8,128)S(1)} %pad_maximum_fusion.1), channel_id=1, source_target_pairs={{0,1},{1,0},{2,3},{3,2},{4,5},{5,4},{6,7},{7,6},{8,9},{9,8},{10,11... | collective-permute-start | bytes 983048 | tf_op jit(solution)/shard_map/ppermute | solution.py:26
  77.8 13.3 %copy-start.5 = (f32[80,8,128]{2,1,0:T(8,128)}, f32[80,8,128]{2,1,0:T(8,128)S(1)}, u32[]{:S(2)}) copy-start(f32[80,8,128]{2,1,0:T(8,128)S(1)} %collective-permute-done.8) | copy-start | bytes 983044
  77.8 14.3 %collective-permute-start.17 = (f32[80,8,128]{2,1,0:T(8,128)S(1)}, f32[80,8,128]{2,1,0:T(8,128)}, u32[]{:S(2)}, u32[]{:S(2)}) collective-permute-start(f32[80,8,128]{2,1,0:T(8,128)S(1)} %pad_maximum_fusion.1), channel_id=1, source_target_pairs={{0,16},{1,17},{2,18},{3,19},{4,20},{5,21},{6,22},{7,23},{8,24},{9,... | collective-permute-start | bytes 983048 | tf_op jit(solution)/shard_map/ppermute | solution.py:26
  79.5 11.6 %copy-start.6 = (f32[80,8,128]{2,1,0:T(8,128)}, f32[80,8,128]{2,1,0:T(8,128)S(1)}, u32[]{:S(2)}) copy-start(f32[80,8,128]{2,1,0:T(8,128)S(1)} %collective-permute-done.7) | copy-start | bytes 983044
  79.5 14.5 %collective-permute-start.16 = (f32[80,8,128]{2,1,0:T(8,128)S(1)}, f32[80,8,128]{2,1,0:T(8,128)}, u32[]{:S(2)}, u32[]{:S(2)}) collective-permute-start(f32[80,8,128]{2,1,0:T(8,128)S(1)} %pad_maximum_fusion.1), channel_id=1, source_target_pairs={{0,24},{1,25},{2,26},{3,27},{4,28},{5,29},{6,30},{7,31},{8,0},{9,1... | collective-permute-start | bytes 983048 | tf_op jit(solution)/shard_map/ppermute | solution.py:26
  80.2 0.8 copy-start.7
  80.2 15.9 %collective-permute-start.15 = (f32[80,8,128]{2,1,0:T(8,128)S(1)}, f32[80,8,128]{2,1,0:T(8,128)}, u32[]{:S(2)}, u32[]{:S(2)}) collective-permute-start(f32[80,8,128]{2,1,0:T(8,128)S(1)} %pad_maximum_fusion.1), channel_id=1, source_target_pairs={{0,8},{1,9},{2,10},{3,11},{4,12},{5,13},{6,14},{7,15},{8,16},{9,17... | collective-permute-start | bytes 983048 | tf_op jit(solution)/shard_map/ppermute | solution.py:26
  81.0 1.0 copy-start.8
  81.0 15.6 %collective-permute-start.11 = (f32[80,8,128]{2,1,0:T(8,128)S(1)}, f32[80,8,128]{2,1,0:T(8,128)}, u32[]{:S(2)}, u32[]{:S(2)}) collective-permute-start(f32[80,8,128]{2,1,0:T(8,128)S(1)} %collective-permute-done.7), channel_id=1, source_target_pairs={{0,1},{1,0},{2,3},{3,2},{4,5},{5,4},{6,7},{7,6},{8,9},{9,8},{10,11... | collective-permute-start | bytes 983048 | tf_op jit(solution)/shard_map/ppermute | solution.py:26
  91.2 12.0 %collective-permute-start.10 = (f32[80,8,128]{2,1,0:T(8,128)}, f32[80,8,128]{2,1,0:T(8,128)S(1)}, u32[]{:S(2)}, u32[]{:S(2)}) collective-permute-start(f32[80,8,128]{2,1,0:T(8,128)} %copy-done.7), channel_id=1, source_target_pairs={{0,1},{1,0},{2,3},{3,2},{4,5},{5,4},{6,7},{7,6},{8,9},{9,8},{10,11... | collective-permute-start | bytes 983048 | tf_op jit(solution)/shard_map/ppermute | solution.py:26
  92.2 11.0 %collective-permute-start.9 = (f32[80,8,128]{2,1,0:T(8,128)}, f32[80,8,128]{2,1,0:T(8,128)S(1)}, u32[]{:S(2)}, u32[]{:S(2)}) collective-permute-start(f32[80,8,128]{2,1,0:T(8,128)} %copy-done.8), channel_id=1, source_target_pairs={{0,1},{1,0},{2,3},{3,2},{4,5},{5,4},{6,7},{7,6},{8,9},{9,8},{10,11... | collective-permute-start | bytes 983048 | tf_op jit(solution)/shard_map/ppermute | solution.py:26
  94.0 9.2 %collective-permute-start.21 = (f32[80,8,128]{2,1,0:T(8,128)}, f32[80,8,128]{2,1,0:T(8,128)}, u32[]{:S(2)}, u32[]{:S(2)}) collective-permute-start(f32[80,8,128]{2,1,0:T(8,128)} %collective-permute-done.17), channel_id=1, source_target_pairs={{0,1},{1,0},{2,3},{3,2},{4,5},{5,4},{6,7},{7,6},{8,9},{9,8},{10,11... | collective-permute-start | bytes 983048 | tf_op jit(solution)/shard_map/ppermute | solution.py:26
  96.1 7.1 %collective-permute-start.20 = (f32[80,8,128]{2,1,0:T(8,128)}, f32[80,8,128]{2,1,0:T(8,128)S(1)}, u32[]{:S(2)}, u32[]{:S(2)}) collective-permute-start(f32[80,8,128]{2,1,0:T(8,128)} %collective-permute-done.16), channel_id=1, source_target_pairs={{0,1},{1,0},{2,3},{3,2},{4,5},{5,4},{6,7},{7,6},{8,9},{9,8},{10,11... | collective-permute-start | bytes 983048 | tf_op jit(solution)/shard_map/ppermute | solution.py:26
  96.6 6.7 %collective-permute-start.19 = (f32[80,8,128]{2,1,0:T(8,128)}, f32[80,8,128]{2,1,0:T(8,128)S(1)}, u32[]{:S(2)}, u32[]{:S(2)}) collective-permute-start(f32[80,8,128]{2,1,0:T(8,128)} %collective-permute-done.15), channel_id=1, source_target_pairs={{0,1},{1,0},{2,3},{3,2},{4,5},{5,4},{6,7},{7,6},{8,9},{9,8},{10,11... | collective-permute-start | bytes 983048 | tf_op jit(solution)/shard_map/ppermute | solution.py:26
  103.2 0.7 copy-start.9
  103.2 0.8 copy-start.10
  103.3 1.0 copy-start.11
  103.3 1.0 copy-start.12
  110.9 1.3 copy-start

commit v3 on v2

--- a/solution.py
+++ b/solution.py
@@ -44,7 +44,7 @@
         packed[p] = tiles[order[p]]
         return carry
 
-    lax.fori_loop(0, packed.shape[0], copy, 0, unroll=16)
+    lax.fori_loop(0, packed.shape[0], copy, 0, unroll=64)
     region = me[0]
     slots = order.shape[0] // 32
 
@@ -97,7 +97,7 @@
 def taper_kernel(half, me, plan, lattice, obs_xy, *refs):
     tapers, place_x, place_y, held, sent = refs[-5:]
     count = plan[COUNT]
-    middle = lax.div(count * 2, 3)
+    middle = lax.div(count, 2)
     start, stop = ((0, middle), (middle, count))[half]
     depth = held.shape[0]
 
@@ -273,7 +273,7 @@
         out[order[p]] = received[p]
         return carry
 
-    lax.fori_loop(0, received.shape[0], copy, 0, unroll=16)
+    lax.fori_loop(0, received.shape[0], copy, 0, unroll=64)
 
 
 VMEM = pl.BlockSpec(memory_space=pltpu.VMEM)

time: 172 us -> 173 us (level)
  transfers between devices with their start and end apart: 23 -> 23, of which waited for: 7 -> 7; matrix products, arithmetic and copies ran while one was open for 1% -> 1% of each run, Pallas kernels for 16% -> 15%
where the time goes in v3:
time: 173 us; the launch traced here: 171 us
  Pallas kernels  50.1 us (29%)
  waiting for transfers between devices  42.6 us (25%)
  starting transfers between devices  38.6 us (22%)
  blocking collectives  33.8 us (20%)
  other arithmetic  3.08 us (2%)
  local copies, waits for them, and re-layouts  2.37 us (1%)
    ppermute x20, waiting for transfers between devices, region_shift(): return lax.ppermute(block, 'region', pairs)  42.6 us
    all_to_all x1, blocking collectives, per_device(): lax.all_to_all(analysis.reshape(tiles, 8, BLOCK_NODES), 'region', split_a...  33.8 us
    ppermute x20, starting transfers between devices, region_shift(): return lax.ppermute(block, 'region', pairs)  24.9 us
    pallas_call x1, Pallas kernels, per_device(): pl.pallas_call(analysis_kernel, out_shape=jax.ShapeDtypeStruct((regions,...  20.1 us
    pallas_call x2, Pallas kernels, per_device(): pl.pallas_call(functools.partial(taper_kernel, half), out_shape=jax.Shape...  15.6 us
    all_to_all x1, starting transfers between devices, per_device(): lax.all_to_all(packed, 'region', split_axis=0, concat_axis=0, tiled=True)  8.28 us
    pallas_call x1, Pallas kernels, per_device(): pl.pallas_call(split_kernel, out_shape=(jax.ShapeDtypeStruct((OBS_EXT, 2...  6.63 us
    pallas_call x1, Pallas kernels, per_device(): pl.pallas_call(pack_kernel, out_shape=(jax.ShapeDtypeStruct((tiles, 8, BL...  4.18 us
  transfers between devices with their start and end apart: 23, of which 7 were waited for; matrix products, arithmetic and copies ran while one was open for 1% of the time, Pallas kernels for 15%

profile of v3, /device:TPU:33, one launch (start us, length us, event | category | flops | bytes accessed | tf_op | source)
XLA Modules:
  0.0 170.8 jit_solution(3606050277035561366)
XLA Ops:
  0.0 0.7 pad_maximum_fusion.3
  0.8 3.5 %collective-permute-start = (f32[2,8,256]{2,1,0:T(8,128)S(1)}, f32[2,8,256]{2,1,0:T(8,128)S(1)}, u32[]{:S(2)}, u32[]{:S(2)}) collective-permute-start(f32[2,8,256]{2,1,0:T(8,128)S(1)} %get-tuple-element.15), channel_id=1, source_target_pairs={{0,32},{32,64},{64,96},{96,128},{128,160},{160,192},{192,224},{1,3... | collective-permute-start | bytes 49160 | tf_op jit(solution)/shard_map/ppermute | solution.py:305
  4.3 1.9 %collective-permute-start.1 = (f32[2,8,256]{2,1,0:T(8,128)S(1)}, f32[2,8,256]{2,1,0:T(8,128)S(1)}, u32[]{:S(2)}, u32[]{:S(2)}) collective-permute-start(f32[2,8,256]{2,1,0:T(8,128)S(1)} %get-tuple-element.16), channel_id=1, source_target_pairs={{32,0},{64,32},{96,64},{128,96},{160,128},{192,160},{224,192},{33,... | collective-permute-start | bytes 49160 | tf_op jit(solution)/shard_map/ppermute | solution.py:306
  6.2 0.7 subtract_add_fusion
  6.9 0.2 convert_reduce_fusion
  7.2 0.7 select_reduce_fusion.order
  7.9 0.6 pad_add_fusion.me
  8.5 4.2 %pack.1 = (f32[512,8,128]{2,1,0:T(8,128)}, s32[768]{0:T(1024)}) custom-call(s32[2]{0:T(128)} %pad_add_fusion.me, s32[512]{0:T(512)} %select_reduce_fusion.order, s32[512]{0:T(512)} %totals.1, s32[16,512]{1,0:T(8,128)} %bitcast.56, f32[512,8,128]{2,1,0:T(8,128)} %bitcast.43), custom_call_target="tpu_custom_call" | custom-call | tf_op jit(solution)/shard_map/pack/pallas_call | solution.py:315
  12.7 0.0 copy-start.3
  12.7 8.3 %all-to-all-start = ((f32[512,8,128]{2,1,0:T(8,128)}), f32[512,8,128]{2,1,0:T(8,128)S(1)}, u32[]{:S(2)}, u32[]{:S(2)}) async-start(f32[512,8,128]{2,1,0:T(8,128)} %get-tuple-element.10), calls=%async_computation | async-start | bytes 4194304 | tf_op jit(solution)/shard_map/all_to_all | solution.py:331
  21.1 3.0 %collective-permute-start.4 = (f32[20,8,128]{2,1,0:T(8,128)S(1)}, f32[20,8,128]{2,1,0:T(8,128)S(1)}, u32[]{:S(2)}, u32[]{:S(2)}) collective-permute-start(f32[20,8,128]{2,1,0:T(8,128)S(1)} %get-tuple-element.14), channel_id=1, source_target_pairs={{0,16},{1,17},{2,18},{3,19},{4,20},{5,21},{6,22},{7,23},{8,24},{9,... | collective-permute-start | bytes 245768 | tf_op jit(solution)/shard_map/ppermute | solution.py:26
  24.0 0.9 collective-permute-start.3
  24.9 0.6 collective-permute-start.2
  25.5 2.7 %collective-permute-start.14 = (f32[20,8,128]{2,1,0:T(8,128)S(1)}, f32[20,8,128]{2,1,0:T(8,128)S(1)}, u32[]{:S(2)}, u32[]{:S(2)}) collective-permute-start(f32[20,8,128]{2,1,0:T(8,128)S(1)} %get-tuple-element.13), channel_id=1, source_target_pairs={{0,4},{1,5},{2,6},{3,7},{4,0},{5,1},{6,2},{7,3},{8,12},{9,13},{10,... | collective-permute-start | bytes 245768 | tf_op jit(solution)/shard_map/ppermute | solution.py:26
  28.2 20.9 %collective-permute-done.4 = f32[20,8,128]{2,1,0:T(8,128)S(1)} collective-permute-done((f32[20,8,128]{2,1,0:T(8,128)S(1)}, f32[20,8,128]{2,1,0:T(8,128)S(1)}, u32[]{:S(2)}, u32[]{:S(2)}) %collective-permute-start.4) | collective-permute-done | bytes 81952 | tf_op jit(solution)/shard_map/ppermute | solution.py:26
  49.1 0.4 collective-permute-done.3
  49.5 0.9 collective-permute-done.2
  50.4 1.1 collective-permute-start.8
  51.5 2.7 %collective-permute-start.7 = (f32[80,8,128]{2,1,0:T(8,128)S(1)}, f32[80,8,128]{2,1,0:T(8,128)S(1)}, u32[]{:S(2)}, u32[]{:S(2)}) collective-permute-start(f32[80,8,128]{2,1,0:T(8,128)S(1)} %pad_maximum_fusion), channel_id=1, source_target_pairs={{0,4},{1,5},{2,6},{3,7},{4,0},{5,1},{6,2},{7,3},{8,12},{9,13},{10,... | collective-permute-start | bytes 983048 | tf_op jit(solution)/shard_map/ppermute | solution.py:26
  54.2 0.9 collective-permute-start.6
  55.0 0.6 collective-permute-start.5
  55.6 2.1 %collective-permute-start.13 = (f32[20,8,128]{2,1,0:T(8,128)S(1)}, f32[20,8,128]{2,1,0:T(8,128)S(1)}, u32[]{:S(2)}, u32[]{:S(2)}) collective-permute-start(f32[20,8,128]{2,1,0:T(8,128)S(1)} %get-tuple-element.13), channel_id=1, source_target_pairs={{0,6},{1,7},{2,0},{3,1},{4,2},{5,3},{6,4},{7,5},{8,14},{9,15},{10,... | collective-permute-start | bytes 245768 | tf_op jit(solution)/shard_map/ppermute | solution.py:26
  57.7 13.3 %collective-permute-done.13 = f32[20,8,128]{2,1,0:T(8,128)S(1)} collective-permute-done((f32[20,8,128]{2,1,0:T(8,128)S(1)}, f32[20,8,128]{2,1,0:T(8,128)S(1)}, u32[]{:S(2)}, u32[]{:S(2)}) %collective-permute-start.13) | collective-permute-done | bytes 81952 | tf_op jit(solution)/shard_map/ppermute | solution.py:26
  71.0 1.6 collective-permute-start.12
  72.6 3.1 %collective-permute-done.12 = f32[20,8,128]{2,1,0:T(8,128)S(1)} collective-permute-done((f32[20,8,128]{2,1,0:T(8,128)S(1)}, f32[20,8,128]{2,1,0:T(8,128)S(1)}, u32[]{:S(2)}, u32[]{:S(2)}) %collective-permute-start.12) | collective-permute-done | bytes 81952 | tf_op jit(solution)/shard_map/ppermute | solution.py:26
  75.7 2.0 %collective-permute-start.18 = (f32[80,8,128]{2,1,0:T(8,128)S(1)}, f32[80,8,128]{2,1,0:T(8,128)}, u32[]{:S(2)}, u32[]{:S(2)}) collective-permute-start(f32[80,8,128]{2,1,0:T(8,128)S(1)} %pad_maximum_fusion.1), channel_id=1, source_target_pairs={{0,1},{1,0},{2,3},{3,2},{4,5},{5,4},{6,7},{7,6},{8,9},{9,8},{10,11... | collective-permute-start | bytes 983048 | tf_op jit(solution)/shard_map/ppermute | solution.py:26
  77.7 1.7 collective-permute-start.17
  79.4 0.6 collective-permute-start.16
  80.1 0.8 collective-permute-start.15
  80.9 1.0 collective-permute-start.11
  81.9 7.8 %shard_map.73.refs_0_ = f32[128,256,128]{2,1,0:T(8,128)} custom-call(s32[2]{0:T(128)} %pad_add_fusion.me, s32[768]{0:T(1024)} %get-tuple-element.9.plan, f32[512,2,128]{2,1,0:T(2,128)} %bitcast.46, f32[128,2,128]{2,1,0:T(2,128)} %bitcast.54), custom_call_target="tpu_custom_call" | custom-call | flops 5000000000 | bytes 4194304 | tf_op jit(solution)/shard_map/pallas_call | solution.py:347
  89.8 0.9 collective-permute-start.10
  90.7 0.3 collective-permute-start.9
  91.0 2.9 %collective-permute-done.16 = f32[80,8,128]{2,1,0:T(8,128)} collective-permute-done((f32[80,8,128]{2,1,0:T(8,128)S(1)}, f32[80,8,128]{2,1,0:T(8,128)}, u32[]{:S(2)}, u32[]{:S(2)}) %collective-permute-start.16) | collective-permute-done | bytes 327712 | tf_op jit(solution)/shard_map/ppermute | solution.py:26
  93.9 1.0 collective-permute-start.21
  94.9 1.1 collective-permute-done.15
  96.0 0.5 collective-permute-start.20
  96.5 0.0 collective-permute-start.19
  96.5 7.8 %shard_map.74.tapers = f32[128,256,128]{2,1,0:T(8,128)} custom-call(s32[2]{0:T(128)} %pad_add_fusion.me, s32[768]{0:T(1024)} %get-tuple-element.9.plan, f32[512,2,128]{2,1,0:T(2,128)} %bitcast.47, f32[128,2,128]{2,1,0:T(2,128)} %bitcast.55, f32[128,256,128]{2,1,0:T(8,128)} %shard_map.73.refs_0_), custom_call_target="tpu_custom_call", output_to_operand_aliasing={{}: (4, {})} | custom-call | flops 5000000000 | bytes 4194304 | tf_op jit(solution)/shard_map/pallas_call | solution.py:347
  104.4 0.6 copy-done.9
  105.1 0.1 copy-done.10
  105.2 0.2 copy-done.11
  105.4 0.1 copy-done.12
  105.4 6.6 %split.1 = (bf16[20,256,256]{2,1,0:T(8,128)(2,1)}, bf16[20,512,128]{2,1,0:T(8,128)(2,1)}) custom-call(f32[4,20,8,128]{3,2,1,0:T(8,128)} %bitcast.48, f32[4,20,8,128]{3,2,1,0:T(8,128)} %bitcast.60, f32[4,20,8,128]{3,2,1,0:T(8,128)} %bitcast.59, f32[4,20,8,128]{3,2,1,0:T(8,128)} %bitcast.58, f32[4,20,8,128]{3,2,1,0:T(8,128)} %bitcast.57, ...), custom_call_target="tpu_custom_call" | custom-call | flops 5000000000 | bytes 10485760 | tf_op jit(solution)/shard_map/split/pallas_call | solution.py:371
  112.1 1.3 copy-done
  113.4 20.1 %analysis.1 = f32[32,16,8,128]{3,2,1,0:T(8,128)} custom-call(s32[768]{0:T(1024)} %get-tuple-element.9.plan, f32[32,16,8,128]{3,2,1,0:T(8,128)} %bitcast.44, bf16[20,256,256]{2,1,0:T(8,128)(2,1)} %get-tuple-element.11.obs_any, bf16[20,512,128]{2,1,0:T(8,128)(2,1)} %get-tuple-element.12.inn_any, f32[128,256,128]{2,1,0:T(8,128)} %shard_map.74.tapers), custom_call_target="tpu_custom_call" | custom-call | flops 20000000000 | bytes 16777216 | tf_op jit(solution)/shard_map/analysis/pallas_call | solution.py:390
  133.6 33.8 %all_to_all.10.received = f32[512,8,128]{2,1,0:T(8,128)} all-to-all(f32[512,8,128]{2,1,0:T(8,128)} %bitcast.45), channel_id=1, replica_groups=mesh['slab'=8,'region'=32] {'region'}, dimensions={0} | all-to-all | bytes 4194304 | tf_op jit(solution)/shard_map/all_to_all | solution.py:409
  167.3 3.5 %unpack.1 = f32[512,8,128]{2,1,0:T(8,128)} custom-call(s32[512]{0:T(512)} %select_reduce_fusion.order, f32[512,8,128]{2,1,0:T(8,128)} %all_to_all.10.received), custom_call_target="tpu_custom_call" | custom-call | tf_op jit(solution)/shard_map/unpack/pallas_call | solution.py:412
  (41 shorter events, 0.2 us)
Async XLA Ops:
  0.8 20.3 %collective-permute-start = (f32[2,8,256]{2,1,0:T(8,128)S(1)}, f32[2,8,256]{2,1,0:T(8,128)S(1)}, u32[]{:S(2)}, u32[]{:S(2)}) collective-permute-start(f32[2,8,256]{2,1,0:T(8,128)S(1)} %get-tuple-element.15), channel_id=1, source_target_pairs={{0,32},{32,64},{64,96},{96,128},{128,160},{160,192},{192,224},{1,3... | collective-permute-start | bytes 49160 | tf_op jit(solution)/shard_map/ppermute | solution.py:305
  4.3 16.7 %collective-permute-start.1 = (f32[2,8,256]{2,1,0:T(8,128)S(1)}, f32[2,8,256]{2,1,0:T(8,128)S(1)}, u32[]{:S(2)}, u32[]{:S(2)}) collective-permute-start(f32[2,8,256]{2,1,0:T(8,128)S(1)} %get-tuple-element.16), channel_id=1, source_target_pairs={{32,0},{64,32},{96,64},{128,96},{160,128},{192,160},{224,192},{33,... | collective-permute-start | bytes 49160 | tf_op jit(solution)/shard_map/ppermute | solution.py:306
  12.7 8.3 %copy-start.3 = (f32[8,2048]{1,0:T(8,128)S(1)}, f32[8,2048]{1,0:T(8,128)}, u32[]{:S(2)}) copy-start(f32[8,2048]{1,0:T(8,128)} %param.9) | copy-start | bytes 196612
  12.7 8.3 %copy-start.4 = (f32[8,2048]{1,0:T(8,128)S(1)}, f32[8,2048]{1,0:T(8,128)}, u32[]{:S(2)}) copy-start(f32[8,2048]{1,0:T(8,128)} %param.8) | copy-start | bytes 196612
  12.7 99.4 %all-to-all-start = ((f32[512,8,128]{2,1,0:T(8,128)}), f32[512,8,128]{2,1,0:T(8,128)S(1)}, u32[]{:S(2)}, u32[]{:S(2)}) async-start(f32[512,8,128]{2,1,0:T(8,128)} %get-tuple-element.10), calls=%async_computation | async-start | bytes 4194304 | tf_op jit(solution)/shard_map/all_to_all | solution.py:331
  21.1 28.0 %collective-permute-start.4 = (f32[20,8,128]{2,1,0:T(8,128)S(1)}, f32[20,8,128]{2,1,0:T(8,128)S(1)}, u32[]{:S(2)}, u32[]{:S(2)}) collective-permute-start(f32[20,8,128]{2,1,0:T(8,128)S(1)} %get-tuple-element.14), channel_id=1, source_target_pairs={{0,16},{1,17},{2,18},{3,19},{4,20},{5,21},{6,22},{7,23},{8,24},{9,... | collective-permute-start | bytes 245768 | tf_op jit(solution)/shard_map/ppermute | solution.py:26
  24.0 25.5 %collective-permute-start.3 = (f32[20,8,128]{2,1,0:T(8,128)S(1)}, f32[20,8,128]{2,1,0:T(8,128)S(1)}, u32[]{:S(2)}, u32[]{:S(2)}) collective-permute-start(f32[20,8,128]{2,1,0:T(8,128)S(1)} %get-tuple-element.14), channel_id=1, source_target_pairs={{0,24},{1,25},{2,26},{3,27},{4,28},{5,29},{6,30},{7,31},{8,0},{9,1... | collective-permute-start | bytes 245768 | tf_op jit(solution)/shard_map/ppermute | solution.py:26
  24.9 25.4 %collective-permute-start.2 = (f32[20,8,128]{2,1,0:T(8,128)S(1)}, f32[20,8,128]{2,1,0:T(8,128)S(1)}, u32[]{:S(2)}, u32[]{:S(2)}) collective-permute-start(f32[20,8,128]{2,1,0:T(8,128)S(1)} %get-tuple-element.14), channel_id=1, source_target_pairs={{0,8},{1,9},{2,10},{3,11},{4,12},{5,13},{6,14},{7,15},{8,16},{9,17... | collective-permute-start | bytes 245768 | tf_op jit(solution)/shard_map/ppermute | solution.py:26
  25.5 30.1 %collective-permute-start.14 = (f32[20,8,128]{2,1,0:T(8,128)S(1)}, f32[20,8,128]{2,1,0:T(8,128)S(1)}, u32[]{:S(2)}, u32[]{:S(2)}) collective-permute-start(f32[20,8,128]{2,1,0:T(8,128)S(1)} %get-tuple-element.13), channel_id=1, source_target_pairs={{0,4},{1,5},{2,6},{3,7},{4,0},{5,1},{6,2},{7,3},{8,12},{9,13},{10,... | collective-permute-start | bytes 245768 | tf_op jit(solution)/shard_map/ppermute | solution.py:26
  50.4 39.4 %copy-start.1 = (f32[80,8,128]{2,1,0:T(8,128)}, f32[80,8,128]{2,1,0:T(8,128)S(1)}, u32[]{:S(2)}) copy-start(f32[80,8,128]{2,1,0:T(8,128)S(1)} %pad_maximum_fusion) | copy-start | bytes 983044
  50.4 27.3 %collective-permute-start.8 = (f32[80,8,128]{2,1,0:T(8,128)S(1)}, f32[80,8,128]{2,1,0:T(8,128)S(1)}, u32[]{:S(2)}, u32[]{:S(2)}) collective-permute-start(f32[80,8,128]{2,1,0:T(8,128)S(1)} %pad_maximum_fusion), channel_id=1, source_target_pairs={{0,1},{1,0},{2,3},{3,2},{4,5},{5,4},{6,7},{7,6},{8,9},{9,8},{10,11... | collective-permute-start | bytes 983048 | tf_op jit(solution)/shard_map/ppermute | solution.py:26
  51.5 28.0 %collective-permute-start.7 = (f32[80,8,128]{2,1,0:T(8,128)S(1)}, f32[80,8,128]{2,1,0:T(8,128)S(1)}, u32[]{:S(2)}, u32[]{:S(2)}) collective-permute-start(f32[80,8,128]{2,1,0:T(8,128)S(1)} %pad_maximum_fusion), channel_id=1, source_target_pairs={{0,4},{1,5},{2,6},{3,7},{4,0},{5,1},{6,2},{7,3},{8,12},{9,13},{10,... | collective-permute-start | bytes 983048 | tf_op jit(solution)/shard_map/ppermute | solution.py:26
  54.2 25.9 %collective-permute-start.6 = (f32[80,8,128]{2,1,0:T(8,128)S(1)}, f32[80,8,128]{2,1,0:T(8,128)S(1)}, u32[]{:S(2)}, u32[]{:S(2)}) collective-permute-start(f32[80,8,128]{2,1,0:T(8,128)S(1)} %pad_maximum_fusion), channel_id=1, source_target_pairs={{0,6},{1,7},{2,0},{3,1},{4,2},{5,3},{6,4},{7,5},{8,14},{9,15},{10,... | collective-permute-start | bytes 983048 | tf_op jit(solution)/shard_map/ppermute | solution.py:26
  55.0 25.8 %collective-permute-start.5 = (f32[80,8,128]{2,1,0:T(8,128)S(1)}, f32[80,8,128]{2,1,0:T(8,128)S(1)}, u32[]{:S(2)}, u32[]{:S(2)}) collective-permute-start(f32[80,8,128]{2,1,0:T(8,128)S(1)} %pad_maximum_fusion), channel_id=1, source_target_pairs={{0,2},{1,3},{2,4},{3,5},{4,6},{5,7},{6,0},{7,1},{8,10},{9,11},{10,... | collective-permute-start | bytes 983048 | tf_op jit(solution)/shard_map/ppermute | solution.py:26
  55.6 15.3 %collective-permute-start.13 = (f32[20,8,128]{2,1,0:T(8,128)S(1)}, f32[20,8,128]{2,1,0:T(8,128)S(1)}, u32[]{:S(2)}, u32[]{:S(2)}) collective-permute-start(f32[20,8,128]{2,1,0:T(8,128)S(1)} %get-tuple-element.13), channel_id=1, source_target_pairs={{0,6},{1,7},{2,0},{3,1},{4,2},{5,3},{6,4},{7,5},{8,14},{9,15},{10,... | collective-permute-start | bytes 245768 | tf_op jit(solution)/shard_map/ppermute | solution.py:26
  71.0 4.7 %collective-permute-start.12 = (f32[20,8,128]{2,1,0:T(8,128)S(1)}, f32[20,8,128]{2,1,0:T(8,128)S(1)}, u32[]{:S(2)}, u32[]{:S(2)}) collective-permute-start(f32[20,8,128]{2,1,0:T(8,128)S(1)} %get-tuple-element.13), channel_id=1, source_target_pairs={{0,2},{1,3},{2,4},{3,5},{4,6},{5,7},{6,0},{7,1},{8,10},{9,11},{10,... | collective-permute-start | bytes 245768 | tf_op jit(solution)/shard_map/ppermute | solution.py:26
  75.7 14.1 %copy-start.2 = (f32[80,8,128]{2,1,0:T(8,128)}, f32[80,8,128]{2,1,0:T(8,128)S(1)}, u32[]{:S(2)}) copy-start(f32[80,8,128]{2,1,0:T(8,128)S(1)} %pad_maximum_fusion.1) | copy-start | bytes 983044
  75.7 14.1 %collective-permute-start.18 = (f32[80,8,128]{2,1,0:T(8,128)S(1)}, f32[80,8,128]{2,1,0:T(8,128)}, u32[]{:S(2)}, u32[]{:S(2)}) collective-permute-start(f32[80,8,128]{2,1,0:T(8,128)S(1)} %pad_maximum_fusion.1), channel_id=1, source_target_pairs={{0,1},{1,0},{2,3},{3,2},{4,5},{5,4},{6,7},{7,6},{8,9},{9,8},{10,11... | collective-permute-start | bytes 983048 | tf_op jit(solution)/shard_map/ppermute | solution.py:26
  77.7 12.1 %copy-start.5 = (f32[80,8,128]{2,1,0:T(8,128)}, f32[80,8,128]{2,1,0:T(8,128)S(1)}, u32[]{:S(2)}) copy-start(f32[80,8,128]{2,1,0:T(8,128)S(1)} %collective-permute-done.8) | copy-start | bytes 983044
  77.7 13.0 %collective-permute-start.17 = (f32[80,8,128]{2,1,0:T(8,128)S(1)}, f32[80,8,128]{2,1,0:T(8,128)}, u32[]{:S(2)}, u32[]{:S(2)}) collective-permute-start(f32[80,8,128]{2,1,0:T(8,128)S(1)} %pad_maximum_fusion.1), channel_id=1, source_target_pairs={{0,16},{1,17},{2,18},{3,19},{4,20},{5,21},{6,22},{7,23},{8,24},{9,... | collective-permute-start | bytes 983048 | tf_op jit(solution)/shard_map/ppermute | solution.py:26
  79.4 10.4 %copy-start.6 = (f32[80,8,128]{2,1,0:T(8,128)}, f32[80,8,128]{2,1,0:T(8,128)S(1)}, u32[]{:S(2)}) copy-start(f32[80,8,128]{2,1,0:T(8,128)S(1)} %collective-permute-done.7) | copy-start | bytes 983044
  79.4 14.5 %collective-permute-start.16 = (f32[80,8,128]{2,1,0:T(8,128)S(1)}, f32[80,8,128]{2,1,0:T(8,128)}, u32[]{:S(2)}, u32[]{:S(2)}) collective-permute-start(f32[80,8,128]{2,1,0:T(8,128)S(1)} %pad_maximum_fusion.1), channel_id=1, source_target_pairs={{0,24},{1,25},{2,26},{3,27},{4,28},{5,29},{6,30},{7,31},{8,0},{9,1... | collective-permute-start | bytes 983048 | tf_op jit(solution)/shard_map/ppermute | solution.py:26
  80.1 0.8 copy-start.7
  80.1 15.9 %collective-permute-start.15 = (f32[80,8,128]{2,1,0:T(8,128)S(1)}, f32[80,8,128]{2,1,0:T(8,128)}, u32[]{:S(2)}, u32[]{:S(2)}) collective-permute-start(f32[80,8,128]{2,1,0:T(8,128)S(1)} %pad_maximum_fusion.1), channel_id=1, source_target_pairs={{0,8},{1,9},{2,10},{3,11},{4,12},{5,13},{6,14},{7,15},{8,16},{9,17... | collective-permute-start | bytes 983048 | tf_op jit(solution)/shard_map/ppermute | solution.py:26
  80.9 1.0 copy-start.8
  80.9 15.6 %collective-permute-start.11 = (f32[80,8,128]{2,1,0:T(8,128)S(1)}, f32[80,8,128]{2,1,0:T(8,128)}, u32[]{:S(2)}, u32[]{:S(2)}) collective-permute-start(f32[80,8,128]{2,1,0:T(8,128)S(1)} %collective-permute-done.7), channel_id=1, source_target_pairs={{0,1},{1,0},{2,3},{3,2},{4,5},{5,4},{6,7},{7,6},{8,9},{9,8},{10,11... | collective-permute-start | bytes 983048 | tf_op jit(solution)/shard_map/ppermute | solution.py:26
  89.8 14.5 %collective-permute-start.10 = (f32[80,8,128]{2,1,0:T(8,128)}, f32[80,8,128]{2,1,0:T(8,128)S(1)}, u32[]{:S(2)}, u32[]{:S(2)}) collective-permute-start(f32[80,8,128]{2,1,0:T(8,128)} %copy-done.7), channel_id=1, source_target_pairs={{0,1},{1,0},{2,3},{3,2},{4,5},{5,4},{6,7},{7,6},{8,9},{9,8},{10,11... | collective-permute-start | bytes 983048 | tf_op jit(solution)/shard_map/ppermute | solution.py:26
  90.7 13.7 %collective-permute-start.9 = (f32[80,8,128]{2,1,0:T(8,128)}, f32[80,8,128]{2,1,0:T(8,128)S(1)}, u32[]{:S(2)}, u32[]{:S(2)}) collective-permute-start(f32[80,8,128]{2,1,0:T(8,128)} %copy-done.8), channel_id=1, source_target_pairs={{0,1},{1,0},{2,3},{3,2},{4,5},{5,4},{6,7},{7,6},{8,9},{9,8},{10,11... | collective-permute-start | bytes 983048 | tf_op jit(solution)/shard_map/ppermute | solution.py:26
  93.9 10.5 %collective-permute-start.21 = (f32[80,8,128]{2,1,0:T(8,128)}, f32[80,8,128]{2,1,0:T(8,128)}, u32[]{:S(2)}, u32[]{:S(2)}) collective-permute-start(f32[80,8,128]{2,1,0:T(8,128)} %collective-permute-done.17), channel_id=1, source_target_pairs={{0,1},{1,0},{2,3},{3,2},{4,5},{5,4},{6,7},{7,6},{8,9},{9,8},{10,11... | collective-permute-start | bytes 983048 | tf_op jit(solution)/shard_map/ppermute | solution.py:26
  96.0 8.4 %collective-permute-start.20 = (f32[80,8,128]{2,1,0:T(8,128)}, f32[80,8,128]{2,1,0:T(8,128)S(1)}, u32[]{:S(2)}, u32[]{:S(2)}) collective-permute-start(f32[80,8,128]{2,1,0:T(8,128)} %collective-permute-done.16), channel_id=1, source_target_pairs={{0,1},{1,0},{2,3},{3,2},{4,5},{5,4},{6,7},{7,6},{8,9},{9,8},{10,11... | collective-permute-start | bytes 983048 | tf_op jit(solution)/shard_map/ppermute | solution.py:26
  96.5 7.9 %collective-permute-start.19 = (f32[80,8,128]{2,1,0:T(8,128)}, f32[80,8,128]{2,1,0:T(8,128)S(1)}, u32[]{:S(2)}, u32[]{:S(2)}) collective-permute-start(f32[80,8,128]{2,1,0:T(8,128)} %collective-permute-done.15), channel_id=1, source_target_pairs={{0,1},{1,0},{2,3},{3,2},{4,5},{5,4},{6,7},{7,6},{8,9},{9,8},{10,11... | collective-permute-start | bytes 983048 | tf_op jit(solution)/shard_map/ppermute | solution.py:26
  104.4 0.7 copy-start.9
  104.4 0.8 copy-start.10
  104.4 1.0 copy-start.11
  104.4 1.0 copy-start.12
  112.1 1.3 copy-start
